TPU v7x, 256 devices: a whole 4x4x8 slice. The times are simulated.
256 devices in a mesh: wide: 32 (over z, x_lo, core), req: 8 (over y, x_hi).
Axes of the slice: x: 4 (x_hi: 2, x_lo: 2; x = x_hi * 2 + x_lo), y: 4, z: 8, core: 2. Of those that a mesh axis runs over, the one named last changes fastest.
Arguments:
- x_in: bfloat16 [2048, 8192], P('req', 'wide'), may hold values from -6 to 6
- w_xz: bfloat16 [8192, 2, 16384], P('req', None, 'wide'), may hold values from -0.0625 to 0.0625
- w_dt: bfloat16 [8192, 256], P('req', 'wide'), may hold values from -0.0625 to 0.0625
- w_bc: bfloat16 [8192, 4096], P('req', 'wide'), may hold values from -0.0625 to 0.0625
- dt_bias: float32 [256], P('wide'), may hold values from -7 to -3
- a_log: float32 [256], P('wide'), may hold values from 0 to 2.77
- d_skip: float32 [256], P('wide'), may hold values from 0.5 to 1.5
- conv_x_w: float32 [4, 16384], P(None, 'wide'), may hold values from -3 to 3
- conv_x_b: float32 [16384], P('wide'), may hold values from -3 to 3
- conv_bc_w: float32 [4, 4096], P(None, 'wide'), may hold values from -3 to 3
- conv_bc_b: float32 [4096], P('wide'), may hold values from -3 to 3
- norm_gain: float32 [16384], P('wide'), may hold values from 0.5 to 1.5
- stretch_start: int32 [8, 2], P('req'), may hold values from 0 to 255, as said below
- prefix_len: int32 [16], P('req'), may hold values from 0 to 32768, as said below
- state_slot: int32 [16], replicated, may hold values from 0 to 63, as said below
- ssm_pool: float32 [64, 256, 64, 256], P('req', 'wide'), may hold values from -6 to 6
- conv_x_pool: bfloat16 [64, 3, 16384], P('req', None, 'wide'), may hold values from -6 to 6
- conv_bc_pool: bfloat16 [64, 3, 4096], P('req', None, 'wide'), may hold values from -6 to 6
Outputs:
- y_out: bfloat16 [2048, 16384], P('req', 'wide')
- new_state: float32 [16, 256, 64, 256], P('req', 'wide')
Inputs may be any that keep to these rules, and one draw needn't show every extreme that they name: `stretch_start`: each row is 0 first and rises strictly; the 2 requests of an index of req cover its 256 tokens in order. `prefix_len`: zero means no cached state; in every draw some request has zero and one has 32768. `state_slot`: distinct slots; slot s is owned by index s // 8 of req; owners hold very uneven numbers of the requested slots.
All inputs are finite; a program needn't handle non-finite values.
Results may differ from a plain program's by a relative error of at most 0.014.
Values may be sent and summed in bfloat16 or wider, within the bound.
A program may use at most 128 MiB of HBM per device.

v0:
```python
import jax
import jax.numpy as jnp
from jax import lax
from jax.sharding import PartitionSpec as P

HEADS = 256
HEAD_DIM = 64
GROUPS = 8


NORM_EPS = 1e-05


def partner_2(block, axis, bit):
    count = lax.axis_size(axis)
    route = []
    for low in range(count):
        high = low | 1 << bit
        if high != low and high < count:
            route += [(low, high), (high, low)]
    return lax.ppermute(block, axis, route)


def segments(starts, count_tok):
    position = jnp.arange(count_tok, dtype=jnp.int32)
    seg_ids = jnp.sum((position[:, None] >= starts[None, :]).astype(jnp.int32), 1) - 1
    member = seg_ids[:, None] == jnp.arange(starts.shape[0], dtype=jnp.int32)[None, :]
    offset = position - jnp.sum(jnp.where(member, starts[None, :], 0), 1)
    same_req = seg_ids[:, None] == seg_ids[None, :]
    causal = position[:, None] >= position[None, :]
    return (member.astype(jnp.float32), offset, (same_req & causal).astype(jnp.float32))


def causal_conv(inputs, cache, kernel, bias, member, offset):
    kernel_len = kernel.shape[0]
    count_tok, channels = inputs.shape
    count_req = cache.shape[0]
    history = jnp.dot(
        member,
        cache.reshape(count_req, (kernel_len - 1) * channels),
        precision=lax.Precision.HIGHEST,
    )
    history = history.reshape(count_tok, kernel_len - 1, channels)
    values = inputs.astype(jnp.float32)
    total = bias[None, :] + kernel[kernel_len - 1][None, :] * values
    for lag_step in range(1, kernel_len):
        shifted = jnp.concatenate(
            [jnp.zeros((lag_step, channels), jnp.float32), values[: count_tok - lag_step]], 0
        )
        earlier = jnp.zeros((count_tok, channels), jnp.float32)
        for slot_place in range(kernel_len - 1):
            hit_place = offset - lag_step + kernel_len - 1 == slot_place
            earlier = earlier + jnp.where(hit_place[:, None], history[:, slot_place], 0.0)
        chosen = jnp.where((offset >= lag_step)[:, None], shifted, earlier)
        total = total + kernel[kernel_len - 1 - lag_step][None, :] * chosen
    return jax.nn.silu(total).astype(jnp.bfloat16)


def mixer(inputs, dt_raw, b_maps, c_maps, start_state, member, mask, dt_bias, a_log, d_skip):
    high = lax.Precision.HIGHEST
    step_size = jax.nn.softplus(dt_raw.astype(jnp.float32) + dt_bias[None, :])
    decay_rate = step_size * (-jnp.exp(a_log))[None, :]
    cumulative = jnp.dot(mask, decay_rate, precision=high)
    scores = jnp.dot(c_maps, b_maps.T, preferred_element_type=jnp.float32)
    spread_gap = jnp.minimum(cumulative.T[:, :, None] - cumulative.T[:, None, :], 0.0)
    decay = jnp.exp(spread_gap) * mask[None] * step_size.T[:, None, :]
    weights = (decay * scores[None]).astype(jnp.bfloat16)
    intra = jnp.einsum("hts,shp->thp", weights, inputs, preferred_element_type=jnp.float32)
    values = inputs.astype(jnp.float32)
    from_state = jnp.einsum(
        "tn,jhpn->jthp", c_maps.astype(jnp.float32), start_state, precision=high
    )
    from_state = jnp.einsum("tj,jthp->thp", member, from_state, precision=high)
    from_state = from_state * jnp.exp(cumulative)[:, :, None]
    result = intra + from_state + d_skip[None, :, None] * values
    ends = jnp.dot(member.T, decay_rate, precision=high)
    to_end = jnp.exp(jnp.dot(member, ends, precision=high) - cumulative)
    carried = (to_end * step_size)[:, :, None] * values
    split_req = (member.T[:, :, None, None] * carried[None]).astype(jnp.bfloat16)
    fresh = jnp.einsum("jthp,tn->jhpn", split_req, b_maps, preferred_element_type=jnp.float32)
    final_state = jnp.exp(ends)[:, :, None, None] * start_state + fresh
    return (result, final_state)


def on_device(
    x_in,
    w_xz,
    w_dt,
    w_bc,
    dt_bias,
    a_log,
    d_skip,
    conv_x_w,
    conv_x_b,
    conv_bc_w,
    conv_bc_b,
    norm_gain,
    stretch_start,
    prefix_len,
    state_slot,
    ssm_pool,
    conv_x_pool,
    conv_bc_pool,
):
    features = lax.all_gather(x_in, "wide", axis=1, tiled=True)
    count_tok = features.shape[0]
    local_width = w_xz.shape[2]
    local_heads = w_dt.shape[1]
    acc_xz = jnp.einsum(
        "td,dkc->tkc",
        features,
        lax.all_gather(w_xz, "req", axis=0, tiled=True),
        preferred_element_type=jnp.float32,
    )
    acc_dt = jnp.dot(
        features,
        lax.all_gather(w_dt, "req", axis=0, tiled=True),
        preferred_element_type=jnp.float32,
    )
    acc_bc = jnp.dot(
        features,
        lax.all_gather(w_bc, "req", axis=0, tiled=True),
        preferred_element_type=jnp.float32,
    )
    proj_xz = acc_xz.astype(jnp.bfloat16)
    dt_raw = acc_dt.astype(jnp.bfloat16)
    bc_raw = acc_bc.astype(jnp.bfloat16)
    owner = lax.axis_index("req")
    req_count = lax.axis_size("req")
    slot_count = conv_x_pool.shape[0]
    local_slot = jnp.clip(state_slot - owner * slot_count, 0, slot_count - 1)
    is_owner = state_slot // slot_count == owner
    send_ssm = jnp.where(is_owner[:, None, None, None], ssm_pool[local_slot], 0.0)
    send_cx = jnp.where(is_owner[:, None, None], conv_x_pool[local_slot].astype(jnp.float32), 0.0)
    send_cbc = jnp.where(is_owner[:, None, None], conv_bc_pool[local_slot].astype(jnp.float32), 0.0)
    got_ssm, got_cx, got_cbc = (
        lax.all_to_all(send_ssm, "req", split_axis=0, concat_axis=0, tiled=True),
        lax.all_to_all(send_cx, "req", split_axis=0, concat_axis=0, tiled=True),
        lax.all_to_all(send_cbc, "req", split_axis=0, concat_axis=0, tiled=True),
    )
    group_reqs = prefix_len.shape[0]
    has_cache = (prefix_len > 0).astype(jnp.float32)
    start_state = (
        jnp.sum(got_ssm.reshape((req_count, group_reqs) + got_ssm.shape[1:]), 0)
        * has_cache[:, None, None, None]
    )
    cache_x = (
        jnp.sum(got_cx.reshape((req_count, group_reqs) + got_cx.shape[1:]), 0)
        * has_cache[:, None, None]
    )
    cache_bc = (
        jnp.sum(got_cbc.reshape((req_count, group_reqs) + got_cbc.shape[1:]), 0)
        * has_cache[:, None, None]
    )
    member, offset, mask = segments(stretch_start[0], count_tok)
    x_conv = causal_conv(proj_xz[:, 1], cache_x, conv_x_w, conv_x_b, member, offset)
    bc_conv = causal_conv(bc_raw, cache_bc, conv_bc_w, conv_bc_b, member, offset)
    wide_index = lax.axis_index("wide")
    group_span = lax.axis_size("wide") // GROUPS
    bit_total = group_span.bit_length() - 1
    joined = bc_conv
    for bit_index in range(bit_total):
        partner = partner_2(joined, "wide", bit_index)
        upper_half = wide_index // (1 << bit_index) % 2 == 1
        joined = jnp.where(
            upper_half, jnp.concatenate([partner, joined], 1), jnp.concatenate([joined, partner], 1)
        )
    state_width = joined.shape[1] // 2
    b_maps = joined[:, :state_width]
    c_maps = joined[:, state_width:]
    head_width = local_width // local_heads
    result, final_state = mixer(
        x_conv.reshape(count_tok, local_heads, head_width),
        dt_raw,
        b_maps,
        c_maps,
        start_state,
        member,
        mask,
        dt_bias,
        a_log,
        d_skip,
    )
    gated = result.reshape(count_tok, local_width) * jax.nn.silu(proj_xz[:, 0].astype(jnp.float32))
    square_sum = jnp.sum(gated * gated, 1)
    for bit_index in range(bit_total):
        square_sum = square_sum + partner_2(square_sum, "wide", bit_index)
    mean_sq = square_sum / (HEADS * HEAD_DIM // GROUPS)
    normed = gated * lax.rsqrt(mean_sq + NORM_EPS)[:, None] * norm_gain[None, :]
    return (normed.astype(jnp.bfloat16), final_state)


def solution(mesh):
    in_specs = (
        P("req", "wide"),
        P("req", None, "wide"),
        P("req", "wide"),
        P("req", "wide"),
        P("wide"),
        P("wide"),
        P("wide"),
        P(None, "wide"),
        P("wide"),
        P(None, "wide"),
        P("wide"),
        P("wide"),
        P("req", None),
        P("req"),
        P(),
        P("req", "wide", None, None),
        P("req", None, "wide"),
        P("req", None, "wide"),
    )
    out_specs = (P("req", "wide"), P("req", "wide", None, None))
    return jax.shard_map(
        on_device, mesh=mesh, in_specs=in_specs, out_specs=out_specs, check_vma=False
    )
```

profile of v0, /device:TPU:101, one launch (start us, length us, event | category | flops | bytes accessed | tf_op | source)
XLA Modules:
  0.0 418.4 jit_solution(5018810072848733110)
XLA Ops:
  8.7 3.2 copy.42
  13.4 6.9 %all-to-all-start.1 = ((f32[16,3,128]{2,1,0:T(4,128)}), f32[16,3,128]{2,1,0:T(4,128)S(1)}, u32[]{:S(2)}, u32[]{:S(2)}) async-start(f32[16,3,128]{2,1,0:T(4,128)} %copy.47), calls=%async_computation.1 | async-start | bytes 65536 | tf_op jit(solution)/shard_map/all_to_all | solution.py:139
  21.8 6.5 %gather_fusion.2 = f32[16,8,64,256]{3,2,1,0:T(8,128)} fusion(f32[8,8,64,256]{3,2,1,0:T(8,128)} %param.33, s32[1024]{0:T(1024)S(1)} %pad_clamp_fusion), kind=kCustom, calls=%fused_computation.2 | custom fusion | bytes 16777280 | tf_op jit(solution)/shard_map/gather | solution.py:133
  28.3 6.6 %all-to-all-start = ((f32[16,3,512]{2,1,0:T(4,128)}), f32[16,3,512]{2,1,0:T(4,128)S(1)}, u32[]{:S(2)}, u32[]{:S(2)}) async-start(f32[16,3,512]{2,1,0:T(4,128)} %copy.43), calls=%async_computation | async-start | bytes 262144 | tf_op jit(solution)/shard_map/all_to_all | solution.py:138
  34.9 8.4 %broadcast_select_fusion = f32[16,8,64,256]{3,2,1,0:T(8,128)} fusion(f32[16,8,64,256]{3,2,1,0:T(8,128)} %gather_fusion.2, pred[16]{0:T(512)(128)(4,1)S(1)} %fusion.71), kind=kLoop, calls=%fused_computation.5 | loop fusion | flops 2097152 | bytes 16777232 | tf_op jit(solution)/shard_map/jit(_where)/select_n | solution.py:133
  43.4 6.8 %all-to-all-start.2 = ((f32[16,8,64,256]{3,2,1,0:T(8,128)}), f32[16,8,64,256]{3,2,1,0:T(8,128)}, u32[]{:S(2)}, u32[]{:S(2)}) async-start(f32[16,8,64,256]{3,2,1,0:T(8,128)} %broadcast_select_fusion), calls=%async_computation.2 | async-start | bytes 16777216 | tf_op jit(solution)/shard_map/all_to_all | solution.py:137
  50.2 123.3 %all_gather.14 = bf16[8192,8]{0,1:T(8,128)(2,1)S(1)} all-gather(bf16[1024,8]{0,1:T(8,128)(2,1)S(1)} %copy-done.4), channel_id=1, replica_groups=mesh['wide'=32,'req'=8] {'req'}, dimensions={0}, use_global_device_ids=true | all-gather | bytes 147456 | tf_op jit(solution)/shard_map/all_gather | solution.py:117
  176.0 4.3 %reduce_sum.64 = f32[2,8,64,256]{3,2,1,0:T(8,128)S(1)} reduce(f32[8,2,8,64,256]{4,3,2,1,0:T(8,128)} %bitcast.33, f32[]{:T(128)} %constant.94.clone.1), dimensions={0}, to_apply=%region_4.5 | reduce | flops 1835008 | bytes 9437188 | tf_op jit(solution)/shard_map/reduce_sum | solution.py:144
  180.4 14.3 %all-gather.4.cloned.1.call-done = bf16[256,8192]{1,0:T(8,128)(2,1)} async-done(((bf16[256,256]{1,0:T(8,128)(2,1)}), bf16[256,8192]{1,0:T(8,128)(2,1)}) %all-gather.4.cloned.1.call-update) | async-done | bytes 4194320 | tf_op jit(solution)/shard_map/all_gather | solution.py:105
  194.7 4.5 %fusion.7 = f32[256,128]{0,1:T(8,128)S(1)} fusion(bf16[256,8192]{1,0:T(8,128)(2,1)} %all-gather.4.cloned.1.call-done, bf16[8192,128]{1,0:T(8,128)(2,1)} %all-gather.8.cloned.1.call-done), kind=kOutput, calls=%fused_computation.13 | convolution fusion | flops 536936448 | bytes 6422528 | tf_op jit(solution)/shard_map/dot_general | solution.py:120
  199.9 1.2 compare_select_fusion
  201.6 1.3 collective-permute-start.1
  203.1 3.6 collective-permute-done.1
  207.5 0.9 fusion.12
  208.5 0.9 fusion.44
  209.4 172.6 %all-gather.6.cloned.1.call-done = bf16[8192,2,512]{2,0,1:T(8,128)(2,1)} async-done(((bf16[1024,2,512]{2,0,1:T(8,128)(2,1)}), bf16[8192,2,512]{2,0,1:T(8,128)(2,1)}) %all-gather.6.cloned.1.call-update) | async-done | bytes 16777232 | tf_op jit(solution)/shard_map/all_gather | solution.py:112
  382.0 11.5 %fusion.2 = bf16[256,2,512]{2,0,1:T(8,128)(2,1)S(1)} fusion(bf16[8192,2,512]{2,0,1:T(8,128)(2,1)} %all-gather.6.cloned.1.call-done, bf16[256,8192]{1,0:T(8,128)(2,1)} %all-gather.4.cloned.1.call-done), kind=kOutput, calls=%fused_computation.8 | convolution fusion | flops 4295229440 | bytes 21495808 | tf_op jit(solution)/shard_map/td,dkc->tkc/dot_general | solution.py:109
  396.9 2.0 copy.52
  399.0 3.0 multiply_convert_fusion.4
  401.9 1.1 copy.46
  403.0 2.2 multiply_reduce_fusion
  405.3 1.5 collective-permute-start.2
  407.6 1.8 collective-permute-start.3
  409.4 1.3 convolution_add_fusion
  (88 shorter events, 14.4 us)
Async XLA Ops:
  7.2 13.1 %copy-start = (bf16[8,3,512]{2,0,1:T(8,128)(2,1)S(1)}, bf16[8,3,512]{2,0,1:T(8,128)(2,1)}, u32[]{:S(2)}) copy-start(bf16[8,3,512]{2,0,1:T(8,128)(2,1)} %param.34) | copy-start | bytes 73732
  7.2 173.2 %all-gather.8.cloned.1.call-start = ((), (), s32[]{:S(2)}) async-start(), calls=%async_computation.5 | async-start | bytes 2359296 | tf_op jit(solution)/shard_map/all_gather | solution.py:122
  7.9 186.7 %all-gather.4.cloned.1.call-start = ((), (), s32[]{:S(2)}) async-start(), calls=%async_computation.3 | async-start | bytes 4325376 | tf_op jit(solution)/shard_map/all_gather | solution.py:105
  8.7 373.3 %all-gather.6.cloned.1.call-start = ((), (), s32[]{:S(2)}) async-start(), calls=%async_computation.4 | async-start | bytes 18874368 | tf_op jit(solution)/shard_map/all_gather | solution.py:112
  13.4 14.9 %all-to-all-start.1 = ((f32[16,3,128]{2,1,0:T(4,128)}), f32[16,3,128]{2,1,0:T(4,128)S(1)}, u32[]{:S(2)}, u32[]{:S(2)}) async-start(f32[16,3,128]{2,1,0:T(4,128)} %copy.47), calls=%async_computation.1 | async-start | bytes 65536 | tf_op jit(solution)/shard_map/all_to_all | solution.py:139
  28.3 15.1 %all-to-all-start = ((f32[16,3,512]{2,1,0:T(4,128)}), f32[16,3,512]{2,1,0:T(4,128)S(1)}, u32[]{:S(2)}, u32[]{:S(2)}) async-start(f32[16,3,512]{2,1,0:T(4,128)} %copy.43), calls=%async_computation | async-start | bytes 262144 | tf_op jit(solution)/shard_map/all_to_all | solution.py:138
  43.3 6.8 %copy-start.4 = (bf16[1024,8]{0,1:T(8,128)(2,1)S(1)}, bf16[1024,8]{0,1:T(8,128)(2,1)}, u32[]{:S(2)}) copy-start(bf16[1024,8]{0,1:T(8,128)(2,1)} %param.20) | copy-start | bytes 49156
  43.3 130.1 %copy-start.11 = (s32[1,2]{1,0:T(1,128)S(1)}, s32[1,2]{1,0:T(1,128)}, u32[]{:S(2)}) copy-start(s32[1,2]{1,0:T(1,128)} %param.30) | copy-start | bytes 28
  43.3 130.3 %copy-start.13 = (s32[2]{0:T(128)S(1)}, s32[2]{0:T(128)}, u32[]{:S(2)}) copy-start(s32[2]{0:T(128)} %param.31) | copy-start | bytes 28
  43.3 130.3 %copy-start.14 = (f32[8]{0:T(128)S(1)}, f32[8]{0:T(128)}, u32[]{:S(2)}) copy-start(f32[8]{0:T(128)} %param.23) | copy-start | bytes 100
  43.4 130.3 %copy-start.9 = (f32[4,128]{1,0:T(4,128)S(1)}, f32[4,128]{1,0:T(4,128)}, u32[]{:S(2)}) copy-start(f32[4,128]{1,0:T(4,128)} %param.27) | copy-start | bytes 6148
  43.4 130.4 %copy-start.5 = (f32[4,512]{1,0:T(4,128)S(1)}, f32[4,512]{1,0:T(4,128)}, u32[]{:S(2)}) copy-start(f32[4,512]{1,0:T(4,128)} %param.25) | copy-start | bytes 24580
  43.4 132.6 %all-to-all-start.2 = ((f32[16,8,64,256]{3,2,1,0:T(8,128)}), f32[16,8,64,256]{3,2,1,0:T(8,128)}, u32[]{:S(2)}, u32[]{:S(2)}) async-start(f32[16,8,64,256]{3,2,1,0:T(8,128)} %broadcast_select_fusion), calls=%async_computation.2 | async-start | bytes 16777216 | tf_op jit(solution)/shard_map/all_to_all | solution.py:137
  180.4 18.8 %copy-start.10 = (f32[128]{0:T(128)S(1)}, f32[128]{0:T(128)}, u32[]{:S(2)}) copy-start(f32[128]{0:T(128)} %param.28) | copy-start | bytes 1540
  180.4 19.5 %copy-start.8 = (f32[8]{0:T(128)S(1)}, f32[8]{0:T(128)}, u32[]{:S(2)}) copy-start(f32[8]{0:T(128)} %param.22) | copy-start | bytes 100
  194.7 5.2 %copy-start.2 = (bf16[256,8192]{1,0:T(8,128)(2,1)S(1)}, bf16[256,8192]{1,0:T(8,128)(2,1)}, u32[]{:S(2)}) copy-start(bf16[256,8192]{1,0:T(8,128)(2,1)} %all-gather.4.cloned.1.call-done) | copy-start | bytes 12582916
  199.5 2.1 collective-permute-start
  201.6 5.1 %collective-permute-start.1 = (bf16[256,256]{0,1:T(8,128)(2,1)S(1)}, bf16[256,256]{0,1:T(8,128)(2,1)S(1)}, u32[]{:S(2)}, u32[]{:S(2)}) collective-permute-start(bf16[256,256]{0,1:T(8,128)(2,1)S(1)} %maximum_select_fusion.1), channel_id=1, source_target_pairs={{0,16},{16,0},{8,24},{24,8},{32,48},{48,32},{40,56},{56,40},{64,80... | collective-permute-start | bytes 393224 | tf_op jit(solution)/shard_map/ppermute | solution.py:21
  393.5 5.4 %copy-start.6 = (f32[512]{0:T(512)S(1)}, f32[512]{0:T(512)}, u32[]{:S(2)}) copy-start(f32[512]{0:T(512)} %param.26) | copy-start | bytes 6148
  394.4 8.6 %copy-start.15 = (f32[8]{0:T(128)S(1)}, f32[8]{0:T(128)}, u32[]{:S(2)}) copy-start(f32[8]{0:T(128)} %param.24) | copy-start | bytes 100
  403.0 7.9 %copy-start.7 = (f32[512]{0:T(512)S(1)}, f32[512]{0:T(512)}, u32[]{:S(2)}) copy-start(f32[512]{0:T(512)} %param.29) | copy-start | bytes 6148
  403.0 8.8 %copy-start.1 = (bf16[8,3,512]{2,0,1:T(8,128)(2,1)S(1)}, bf16[8,3,512]{2,0,1:T(8,128)(2,1)}, u32[]{:S(2)}) copy-start(bf16[8,3,512]{2,0,1:T(8,128)(2,1)} %param.34) | copy-start | bytes 73732
  405.3 2.3 collective-permute-start.2
  407.6 3.3 collective-permute-start.3
  (2 other events, 9.7 us)
Sparse Core Ops, SparseCore 0:
  10.7 80.6 all-gather.7
  93.1 101.5 all-gather.3
  197.3 184.6 all-gather.5
where the time goes:
time: 422 us; the launch traced here: 418 us
  waiting for transfers between devices  193 us (46%)
  blocking collectives  123 us (29%)
  starting transfers between devices  25.3 us (6%)
  matrix products  24.4 us (6%)
  other arithmetic  20.3 us (5%)
  local copies, waits for them, and re-layouts  18.4 us (4%)
  between operations  14.1 us (3%)
    all_gather x1, waiting for transfers between devices, on_device(): lax.all_gather(w_xz, 'req', axis=0, tiled=True)  173 us
    all_gather x1, blocking collectives, on_device(): lax.all_gather(w_dt, 'req', axis=0, tiled=True)  123 us
    all_gather x1, waiting for transfers between devices, on_device(): features = lax.all_gather(x_in, 'wide', axis=1, tiled=True)  14.3 us
    dot_general x1, matrix products, on_device(): jnp.einsum('td,dkc->tkc', features, lax.all_gather(w_xz, 'req', axis=0, t...  11.5 us
  transfers between devices with their start and end apart: 10, of which 4 were waited for; matrix products, arithmetic and copies ran while one was open for 9% of the time, Pallas kernels for 0%

commit v1 on v0

--- a/solution.py
+++ b/solution.py
@@ -1,14 +1,19 @@
+import functools
+
 import jax
 import jax.numpy as jnp
 from jax import lax
+from jax.experimental import pallas as pl
+from jax.experimental.pallas import tpu as pltpu
 from jax.sharding import PartitionSpec as P
 
 HEADS = 256
 HEAD_DIM = 64
 GROUPS = 8
-
-
 NORM_EPS = 1e-05
+MESH = pl.DeviceIdType.MESH
+BF = jnp.bfloat16
+F32 = jnp.float32
 
 
 def partner_2(block, axis, bit):
@@ -82,76 +87,265 @@
     return (result, final_state)
 
 
+ORDER = (0, 2, 1, 3)
+STEPS = ((0,), (1, 7), (2, 6), (3, 5), (4,))
+
+
+def project_kernel(
+    x_ref, wxz_ref, wbd_ref, slot_ref, pool_hbm, cpool_ref,
+    xz_out, bc_out, dt_out, h0_out, cc_out,
+    xg, sbuf, rbuf, sdt, rdt, pool, st_s, st_r, cc_s, cc_r,
+    pool_sem, q_send, q_recv, p_send, p_recv, d_send, d_recv, s_send, s_recv, c_send, c_recv,
+):
+    r = lax.axis_index("req")
+    w = lax.axis_index("wide")
+    z = w // 4
+    j = w % 4
+
+    def wide_at(zz, jj):
+        return zz * 4 + jj
+
+    core_w = wide_at(z, j + 1 - 2 * (j % 2))
+    side_w = wide_at(z, (j + 2) % 4)
+    up_w = wide_at((z + 1) % 8, j)
+    down_w = wide_at((z + 7) % 8, j)
+
+    def xor8(a, v):
+        out = 0
+        for bit in range(3):
+            p = 1 << bit
+            ab = a // p % 2
+            vb = v // p % 2
+            out = out + p * ((ab + vb) % 2)
+        return out
+
+    pool_copy = pltpu.make_async_copy(pool_hbm, pool, pool_sem)
+    pool_copy.start()
+
+    barrier = pltpu.get_barrier_semaphore()
+    for ww in (core_w, side_w, up_w, down_w):
+        pl.semaphore_signal(barrier, inc=1, device_id={"req": r, "wide": ww}, device_id_type=MESH)
+    for v in range(1, 8):
+        pl.semaphore_signal(
+            barrier, inc=1, device_id={"req": xor8(r, v), "wide": w}, device_id_type=MESH
+        )
+    pl.semaphore_wait(barrier, 11)
+
+    counter = [0]
+
+    def send(src, dst, ww):
+        i = counter[0]
+        counter[0] += 1
+        copy = pltpu.make_async_remote_copy(
+            src_ref=src, dst_ref=dst, send_sem=q_send.at[i], recv_sem=q_recv.at[i],
+            device_id={"req": r, "wide": ww}, device_id_type=MESH,
+        )
+        copy.start()
+        return copy
+
+    copies = []
+
+    def go(src, dst, ww):
+        copy = send(src, dst, ww)
+        copies.append(copy)
+        return copy
+
+    side = go(x_ref, xg.at[0, 1], side_w)
+    up0 = go(x_ref, xg.at[1, 0], up_w)
+    down0 = go(x_ref, xg.at[7, 0], down_w)
+    core0 = go(x_ref, xg.at[0, 2], core_w)
+    xg[0, 0] = x_ref[...]
+
+    side.wait_recv()
+    up1 = go(xg.at[0, 1], xg.at[1, 1], up_w)
+    down1 = go(xg.at[0, 1], xg.at[7, 1], down_w)
+    core1 = go(xg.at[0, 1], xg.at[0, 3], core_w)
+
+    pool_copy.wait()
+
+    def state_block(v, i):
+        q = xor8(r, v) * 2 + i
+        slot = slot_ref[q]
+        mine = slot // 8 == r
+        local = jnp.clip(slot - r * 8, 0, 7)
+        return mine, local
+
+    def fill_state(v):
+        m0, l0 = state_block(v, 0)
+        m1, l1 = state_block(v, 1)
+        st_s[v, 0] = jnp.where(m0, pool[l0], 0.0).astype(BF)
+        st_s[v, 1] = jnp.where(m1, pool[l1], 0.0).astype(BF)
+        cc_s[v] = jnp.where(m0, cpool_ref[l0, 0], 0.0) + jnp.where(m1, cpool_ref[l1, 1], 0.0)
+
+    def plane_copy(src, dst, ssem, rsem, v):
+        return pltpu.make_async_remote_copy(
+            src_ref=src, dst_ref=dst, send_sem=ssem, recv_sem=rsem,
+            device_id={"req": xor8(r, v), "wide": w}, device_id_type=MESH,
+        )
+
+    for v in (1, 2, 3, 4, 5, 6, 7, 0):
+        fill_state(v)
+        if v:
+            plane_copy(st_s.at[v], st_r.at[v], s_send.at[v], s_recv.at[v], v).start()
+            plane_copy(cc_s.at[v], cc_r.at[v], c_send.at[v], c_recv.at[v], v).start()
+
+    rows = [pl.multiple_of(xor8(j, q) * 256, 256) for q in ORDER]
+
+    def compute(k):
+        zp = (z + 8 - k) % 8
+        blocks = [xg[k, p] for p in range(4)]
+        for part in range(3):
+            def weights(p):
+                if part < 2:
+                    return wxz_ref[part, pl.ds(rows[p], 256), :]
+                return wbd_ref[pl.ds(rows[p], 256), :]
+
+            acc = jnp.dot(blocks[0], weights(0), preferred_element_type=F32)
+            for p in range(1, 4):
+                acc = acc + jnp.dot(blocks[p], weights(p), preferred_element_type=F32)
+            if part < 2:
+                sbuf[zp, :, part * 512 : part * 512 + 512] = acc.astype(BF)
+            else:
+                sbuf[zp, :, 1024:1152] = acc[:, :128].astype(BF)
+                sdt[zp] = acc[:, 128:].T[:8]
+
+        @pl.when(zp != 0)
+        def _():
+            dest = xor8(r, zp)
+            for src, dst, ssem, rsem in (
+                (sbuf, rbuf, p_send, p_recv), (sdt, rdt, d_send, d_recv),
+            ):
+                pltpu.make_async_remote_copy(
+                    src_ref=src.at[zp], dst_ref=dst.at[zp], send_sem=ssem.at[zp], recv_sem=rsem.at[zp],
+                    device_id={"req": dest, "wide": w}, device_id_type=MESH,
+                ).start()
+
+    core0.wait_recv()
+    core1.wait_recv()
+    arrived = {1: (up0, up1), 7: (down0, down1)}
+    for step in range(len(STEPS)):
+        nxt = STEPS[step + 1] if step + 1 < len(STEPS) else ()
+        partner = {}
+        later = {}
+        for k in nxt:
+            for copy in arrived[k]:
+                copy.wait_recv()
+            partner[k] = go(xg.at[k, 0:2], xg.at[k, 2:4], core_w)
+            if k in (1, 2):
+                later[k + 1] = (go(xg.at[k, 0:2], xg.at[k + 1, 0:2], up_w),)
+            elif k in (7, 6):
+                later[k - 1] = (go(xg.at[k, 0:2], xg.at[k - 1, 0:2], down_w),)
+            elif k == 3:
+                later.setdefault(4, ())
+                later[4] += (go(xg.at[3, 0], xg.at[4, 0], up_w),)
+            elif k == 5:
+                later.setdefault(4, ())
+                later[4] += (go(xg.at[5, 1], xg.at[4, 1], down_w),)
+        arrived = later
+        for k in STEPS[step]:
+            compute(k)
+        for k in nxt:
+            partner[k].wait_recv()
+
+    for copy in copies:
+        copy.wait_send()
+    for v in range(1, 8):
+        for src, dst, ssem, rsem in (
+            (sbuf, rbuf, p_send, p_recv), (sdt, rdt, d_send, d_recv),
+            (st_s, st_r, s_send, s_recv), (cc_s, cc_r, c_send, c_recv),
+        ):
+            plane_copy(src.at[v], dst.at[v], ssem.at[v], rsem.at[v], v).wait()
+
+    total = sbuf[0].astype(F32)
+    dts = sdt[0]
+    caches = cc_s[0]
+    for v in range(1, 8):
+        total = total + rbuf[v].astype(F32)
+        dts = dts + rdt[v]
+        caches = caches + cc_r[v]
+    xz_out[...] = total[:, :1024].astype(BF)
+    bc_out[...] = total[:, 1024:].astype(BF)
+    dt_out[...] = dts
+    cc_out[...] = caches
+    for i in range(2):
+        state = st_s[0, i].astype(F32)
+        for v in range(1, 8):
+            state = state + st_r[v, i].astype(F32)
+        h0_out[i] = state
+
+
+def project(x_t, wxz, wbd, slots, pool, cpool):
+    vm = pl.BlockSpec(memory_space=pltpu.VMEM)
+    dma = pltpu.SemaphoreType.DMA
+    n_q = 7 + 7 + 6
+    return pl.pallas_call(
+        project_kernel,
+        out_shape=(
+            jax.ShapeDtypeStruct((256, 1024), BF),
+            jax.ShapeDtypeStruct((256, 128), BF),
+            jax.ShapeDtypeStruct((8, 256), F32),
+            jax.ShapeDtypeStruct((2, 512, 256), F32),
+            jax.ShapeDtypeStruct((8, 640), F32),
+        ),
+        in_specs=[
+            vm, vm, vm,
+            pl.BlockSpec(memory_space=pltpu.SMEM),
+            pl.BlockSpec(memory_space=pl.ANY),
+            vm,
+        ],
+        out_specs=(vm,) * 5,
+        scratch_shapes=[
+            pltpu.VMEM((8, 4, 256, 256), BF),
+            pltpu.VMEM((8, 256, 1152), BF),
+            pltpu.VMEM((8, 256, 1152), BF),
+            pltpu.VMEM((8, 8, 256), F32),
+            pltpu.VMEM((8, 8, 256), F32),
+            pltpu.VMEM((8, 512, 256), F32),
+            pltpu.VMEM((8, 2, 512, 256), BF),
+            pltpu.VMEM((8, 2, 512, 256), BF),
+            pltpu.VMEM((8, 8, 640), F32),
+            pltpu.VMEM((8, 8, 640), F32),
+            dma(()),
+            dma((n_q,)), dma((n_q,)),
+            dma((8,)), dma((8,)), dma((8,)), dma((8,)),
+            dma((8,)), dma((8,)), dma((8,)), dma((8,)),
+        ],
+        compiler_params=pltpu.CompilerParams(
+            collective_id=0, has_side_effects=True, vmem_limit_bytes=50 << 20
+        ),
+        name="project",
+    )(x_t, wxz, wbd, slots, pool, cpool)
+
+
 def on_device(
-    x_in,
-    w_xz,
-    w_dt,
-    w_bc,
-    dt_bias,
-    a_log,
-    d_skip,
-    conv_x_w,
-    conv_x_b,
-    conv_bc_w,
-    conv_bc_b,
-    norm_gain,
-    stretch_start,
-    prefix_len,
-    state_slot,
-    ssm_pool,
-    conv_x_pool,
-    conv_bc_pool,
+    x_in, w_xz, w_dt, w_bc, dt_bias, a_log, d_skip, conv_x_w, conv_x_b, conv_bc_w, conv_bc_b,
+    norm_gain, stretch_start, prefix_len, state_slot, ssm_pool, conv_x_pool, conv_bc_pool,
 ):
-    features = lax.all_gather(x_in, "wide", axis=1, tiled=True)
-    count_tok = features.shape[0]
-    local_width = w_xz.shape[2]
-    local_heads = w_dt.shape[1]
-    acc_xz = jnp.einsum(
-        "td,dkc->tkc",
-        features,
-        lax.all_gather(w_xz, "req", axis=0, tiled=True),
-        preferred_element_type=jnp.float32,
-    )
-    acc_dt = jnp.dot(
-        features,
-        lax.all_gather(w_dt, "req", axis=0, tiled=True),
-        preferred_element_type=jnp.float32,
-    )
-    acc_bc = jnp.dot(
-        features,
-        lax.all_gather(w_bc, "req", axis=0, tiled=True),
-        preferred_element_type=jnp.float32,
-    )
-    proj_xz = acc_xz.astype(jnp.bfloat16)
-    dt_raw = acc_dt.astype(jnp.bfloat16)
-    bc_raw = acc_bc.astype(jnp.bfloat16)
-    owner = lax.axis_index("req")
-    req_count = lax.axis_size("req")
-    slot_count = conv_x_pool.shape[0]
-    local_slot = jnp.clip(state_slot - owner * slot_count, 0, slot_count - 1)
-    is_owner = state_slot // slot_count == owner
-    send_ssm = jnp.where(is_owner[:, None, None, None], ssm_pool[local_slot], 0.0)
-    send_cx = jnp.where(is_owner[:, None, None], conv_x_pool[local_slot].astype(jnp.float32), 0.0)
-    send_cbc = jnp.where(is_owner[:, None, None], conv_bc_pool[local_slot].astype(jnp.float32), 0.0)
-    got_ssm, got_cx, got_cbc = (
-        lax.all_to_all(send_ssm, "req", split_axis=0, concat_axis=0, tiled=True),
-        lax.all_to_all(send_cx, "req", split_axis=0, concat_axis=0, tiled=True),
-        lax.all_to_all(send_cbc, "req", split_axis=0, concat_axis=0, tiled=True),
-    )
-    group_reqs = prefix_len.shape[0]
-    has_cache = (prefix_len > 0).astype(jnp.float32)
-    start_state = (
-        jnp.sum(got_ssm.reshape((req_count, group_reqs) + got_ssm.shape[1:]), 0)
-        * has_cache[:, None, None, None]
-    )
-    cache_x = (
-        jnp.sum(got_cx.reshape((req_count, group_reqs) + got_cx.shape[1:]), 0)
-        * has_cache[:, None, None]
-    )
-    cache_bc = (
-        jnp.sum(got_cbc.reshape((req_count, group_reqs) + got_cbc.shape[1:]), 0)
-        * has_cache[:, None, None]
-    )
+    route = []
+    for r in range(8):
+        for w in range(32):
+            f, j = w // 4, w % 4
+            route.append((w * 8 + r, ((r ^ f) * 4 + j) * 8 + f))
+    x_t = lax.ppermute(x_in, ("wide", "req"), route)
+    wxz = jnp.transpose(w_xz, (1, 0, 2))
+    wbd = jnp.concatenate([w_bc, w_dt, jnp.zeros((1024, 120), BF)], 1)
+    cp = jnp.concatenate([conv_x_pool, conv_bc_pool], 2).astype(F32)
+    cpool = jnp.stack(
+        [jnp.pad(cp, ((0, 0), (0, 5), (0, 0))), jnp.pad(cp, ((0, 0), (3, 2), (0, 0)))], 1
+    )
+    xz, bc_raw, dt_t, h0, caches = project(
+        x_t, wxz, wbd, state_slot, ssm_pool.reshape(8, 512, 256), cpool
+    )
+    proj_xz = xz.reshape(256, 2, 512)
+    dt_raw = dt_t.T.astype(BF)
+    has_cache = (prefix_len > 0).astype(F32)
+    start_state = h0.reshape(2, 8, 64, 256) * has_cache[:, None, None, None]
+    both = caches[:6].reshape(2, 3, 640) * has_cache[:, None, None]
+    cache_x = both[:, :, :512]
+    cache_bc = both[:, :, 512:]
+    count_tok = 256
+    local_heads = 8
+    local_width = 512
     member, offset, mask = segments(stretch_start[0], count_tok)
     x_conv = causal_conv(proj_xz[:, 1], cache_x, conv_x_w, conv_x_b, member, offset)
     bc_conv = causal_conv(bc_raw, cache_bc, conv_bc_w, conv_bc_b, member, offset)
@@ -171,15 +365,7 @@
     head_width = local_width // local_heads
     result, final_state = mixer(
         x_conv.reshape(count_tok, local_heads, head_width),
-        dt_raw,
-        b_maps,
-        c_maps,
-        start_state,
-        member,
-        mask,
-        dt_bias,
-        a_log,
-        d_skip,
+        dt_raw, b_maps, c_maps, start_state, member, mask, dt_bias, a_log, d_skip,
     )
     gated = result.reshape(count_tok, local_width) * jax.nn.silu(proj_xz[:, 0].astype(jnp.float32))
     square_sum = jnp.sum(gated * gated, 1)
@@ -192,24 +378,10 @@
 
 def solution(mesh):
     in_specs = (
-        P("req", "wide"),
-        P("req", None, "wide"),
-        P("req", "wide"),
-        P("req", "wide"),
-        P("wide"),
-        P("wide"),
-        P("wide"),
-        P(None, "wide"),
-        P("wide"),
-        P(None, "wide"),
-        P("wide"),
-        P("wide"),
-        P("req", None),
-        P("req"),
-        P(),
-        P("req", "wide", None, None),
-        P("req", None, "wide"),
-        P("req", None, "wide"),
+        P("req", "wide"), P("req", None, "wide"), P("req", "wide"), P("req", "wide"),
+        P("wide"), P("wide"), P("wide"), P(None, "wide"), P("wide"), P(None, "wide"),
+        P("wide"), P("wide"), P("req", None), P("req"), P(),
+        P("req", "wide", None, None), P("req", None, "wide"), P("req", None, "wide"),
     )
     out_specs = (P("req", "wide"), P("req", "wide", None, None))
     return jax.shard_map(

time: 422 us -> 181 us (0.43)
  the two profiles are of different devices: /device:TPU:101 before, /device:TPU:240 now
where the time goes in v1:
time: 181 us; the launch traced here: 180 us
  Pallas kernels  134 us (74%)
  local copies, waits for them, and re-layouts  12.6 us (7%)
  other arithmetic  11.3 us (6%)
  starting transfers between devices  9.26 us (5%)
  matrix products  6.21 us (3%)
  waiting for transfers between devices  5.85 us (3%)
    pallas_call x1, Pallas kernels, project(): pl.pallas_call(project_kernel, out_shape=(jax.ShapeDtypeStruct((256, 1024...  134 us
    ppermute x1, starting transfers between devices, on_device(): x_t = lax.ppermute(x_in, ('wide', 'req'), route)  6.53 us
    ppermute x4, waiting for transfers between devices, partner_2(): return lax.ppermute(block, axis, route)  5.84 us
    unnamed x64, local copies, waits for them, and re-layouts  5.77 us
  transfers between devices with their start and end apart: 5, of which 3 were waited for; matrix products, arithmetic and copies ran while one was open for 11% of the time, Pallas kernels for 0%

profile of v1, /device:TPU:240, one launch (start us, length us, event | category | flops | bytes accessed | tf_op | source)
XLA Modules:
  0.0 180.2 jit_solution(426467585842187140)
XLA Ops:
  0.6 6.5 %collective-permute-start = (bf16[256,256]{1,0:T(8,128)(2,1)}, bf16[256,256]{1,0:T(8,128)(2,1)S(1)}, u32[]{:S(2)}, u32[]{:S(2)}) collective-permute-start(bf16[256,256]{1,0:T(8,128)(2,1)} %param.18), channel_id=1, source_target_pairs={{0,0},{8,8},{16,16},{24,24},{32,33},{40,41},{48,49},{56,57},{64,66... | collective-permute-start | bytes 393224 | tf_op jit(solution)/shard_map/ppermute | solution.py:329
  9.2 0.8 fusion.29
  11.6 0.9 copy.36
  13.2 1.5 fusion.63
  15.3 0.8 slice_bitcast_fusion.14
  16.3 1.1 maximum_maximum_fusion.wbd_ref
  17.4 3.3 %copy.76 = bf16[1024,2,512]{2,0,1:T(8,128)(2,1)} copy(bf16[1024,2,512]{2,1,0:T(2,128)(2,1)} %param.19) | data formatting | bytes 4194304 | tf_op args[1]
  20.8 133.6 %project.1 = (bf16[256,1024]{1,0:T(8,128)(2,1)S(1)}, bf16[256,128]{1,0:T(8,128)(2,1)S(1)}, f32[8,256]{1,0:T(8,128)S(1)}, f32[2,512,256]{2,1,0:T(8,128)S(1)}, f32[8,640]{1,0:T(8,128)S(1)}) custom-call(bf16[256,256]{1,0:T(8,128)(2,1)S(1)} %collective-permute-done.x_ref, bf16[2,1024,512]{2,1,0:T(8,128)(2,1)} %bitcast.175, ...), custom_call_target="tpu_custom_call" | custom-call | tf_op jit(solution)/shard_map/project/pallas_call | solution.py:281
  155.5 0.9 copy_convert_fusion
  156.4 0.8 slice_bitcast_fusion.1
  157.3 0.9 slice_bitcast_fusion.5
  158.1 0.9 fusion.64
  160.0 0.8 fusion.52
  161.4 0.9 multiply_convert_fusion.7
  162.4 2.2 %multiply_convert_fusion.6 = bf16[256,512]{1,0:T(8,128)(2,1)S(1)} fusion(f32[253,512]{1,0:T(8,128)S(1)} %slice_bitcast_fusion, f32[254,512]{1,0:T(8,128)S(1)} %copy-done.1, f32[256,3,512]{2,0,1:T(8,128)S(1)} %fusion.52, f32[255,512]{1,0:T(8,128)S(1)} %copy-done.2, f32[512]{0:T(512)} %bitcast.183, f32[512]{0:T(512)} %bitcast.184, f32[512]{0:T(512)} %bitcast.182, ...), kind=kLoop, calls=%fused_computation.47 | loop fusion | flops 4194304 | bytes 3671040 | tf_op jit(solution)/shard_map/convert_element_type | solution.py:61
  165.0 1.2 copy.47
  166.3 1.3 collective-permute-start.2
  168.4 3.9 %collective-permute-done.2 = bf16[256,256]{1,0:T(8,128)(2,1)S(1)} collective-permute-done((bf16[256,256]{1,0:T(8,128)(2,1)S(1)}, bf16[256,256]{1,0:T(8,128)(2,1)S(1)}, u32[]{:S(2)}, u32[]{:S(2)}) %collective-permute-start.2) | collective-permute-done | bytes 131104 | tf_op jit(solution)/shard_map/ppermute | solution.py:26
  173.6 0.9 multiply_reduce_fusion
  174.6 1.1 collective-permute-done.3
  175.7 1.2 collective-permute-start.4
  176.9 1.3 multiply_add_fusion
  178.4 0.9 collective-permute-done.4
  179.3 0.9 fusion.27
  (101 shorter events, 10.3 us)
Async XLA Ops:
  0.6 20.1 %collective-permute-start = (bf16[256,256]{1,0:T(8,128)(2,1)}, bf16[256,256]{1,0:T(8,128)(2,1)S(1)}, u32[]{:S(2)}, u32[]{:S(2)}) collective-permute-start(bf16[256,256]{1,0:T(8,128)(2,1)} %param.18), channel_id=1, source_target_pairs={{0,0},{8,8},{16,16},{24,24},{32,33},{40,41},{48,49},{56,57},{64,66... | collective-permute-start | bytes 393224 | tf_op jit(solution)/shard_map/ppermute | solution.py:329
  10.1 151.2 %copy-start.7 = (pred[256]{0:T(512)(128)(4,1)}, pred[256]{0:T(512)(128)(4,1)S(1)}, u32[]{:S(2)}) copy-start(pred[256]{0:T(512)(128)(4,1)S(1)} %get-tuple-element.24) | copy-start | bytes 772
  10.1 151.2 %copy-start.8 = (pred[256]{0:T(512)(128)(4,1)}, pred[256]{0:T(512)(128)(4,1)S(1)}, u32[]{:S(2)}) copy-start(pred[256]{0:T(512)(128)(4,1)S(1)} %get-tuple-element.25) | copy-start | bytes 772
  10.1 151.2 %copy-start.9 = (pred[256]{0:T(512)(128)(4,1)}, pred[256]{0:T(512)(128)(4,1)S(1)}, u32[]{:S(2)}) copy-start(pred[256]{0:T(512)(128)(4,1)S(1)} %get-tuple-element.26) | copy-start | bytes 772
  10.1 151.2 %copy-start.10 = (pred[256]{0:T(512)(128)(4,1)}, pred[256]{0:T(512)(128)(4,1)S(1)}, u32[]{:S(2)}) copy-start(pred[256]{0:T(512)(128)(4,1)S(1)} %get-tuple-element.27) | copy-start | bytes 772
  10.1 151.2 %copy-start.11 = (pred[256]{0:T(512)(128)(4,1)}, pred[256]{0:T(512)(128)(4,1)S(1)}, u32[]{:S(2)}) copy-start(pred[256]{0:T(512)(128)(4,1)S(1)} %get-tuple-element.28) | copy-start | bytes 772
  10.1 151.2 %copy-start.12 = (pred[256]{0:T(512)(128)(4,1)}, pred[256]{0:T(512)(128)(4,1)S(1)}, u32[]{:S(2)}) copy-start(pred[256]{0:T(512)(128)(4,1)S(1)} %get-tuple-element.29) | copy-start | bytes 772
  10.1 151.2 %copy-start.13 = (pred[256]{0:T(512)(128)(4,1)}, pred[256]{0:T(512)(128)(4,1)S(1)}, u32[]{:S(2)}) copy-start(pred[256]{0:T(512)(128)(4,1)S(1)} %get-tuple-element.30) | copy-start | bytes 772
  10.1 151.2 %copy-start.14 = (pred[256]{0:T(512)(128)(4,1)}, pred[256]{0:T(512)(128)(4,1)S(1)}, u32[]{:S(2)}) copy-start(pred[256]{0:T(512)(128)(4,1)S(1)} %get-tuple-element.31) | copy-start | bytes 772
  10.1 151.2 %copy-start.15 = (pred[256]{0:T(512)(128)(4,1)}, pred[256]{0:T(512)(128)(4,1)S(1)}, u32[]{:S(2)}) copy-start(pred[256]{0:T(512)(128)(4,1)S(1)} %get-tuple-element.32) | copy-start | bytes 772
  10.1 151.2 %copy-start.16 = (pred[256]{0:T(512)(128)(4,1)}, pred[256]{0:T(512)(128)(4,1)S(1)}, u32[]{:S(2)}) copy-start(pred[256]{0:T(512)(128)(4,1)S(1)} %get-tuple-element.33) | copy-start | bytes 772
  10.2 151.2 %copy-start.17 = (pred[256]{0:T(512)(128)(4,1)}, pred[256]{0:T(512)(128)(4,1)S(1)}, u32[]{:S(2)}) copy-start(pred[256]{0:T(512)(128)(4,1)S(1)} %get-tuple-element.34) | copy-start | bytes 772
  10.2 151.2 %copy-start.18 = (pred[256]{0:T(512)(128)(4,1)}, pred[256]{0:T(512)(128)(4,1)S(1)}, u32[]{:S(2)}) copy-start(pred[256]{0:T(512)(128)(4,1)S(1)} %get-tuple-element.35) | copy-start | bytes 772
  13.2 146.7 %copy-start.5 = (f32[2]{0:T(128)}, f32[2]{0:T(128)S(1)}, u32[]{:S(2)}) copy-start(f32[2]{0:T(128)S(1)} %compare_convert_fusion.2) | copy-start | bytes 28
  157.3 4.1 %copy-start.21 = (f32[128]{0:T(128)S(1)}, f32[128]{0:T(128)}, u32[]{:S(2)}) copy-start(f32[128]{0:T(128)} %param.28) | copy-start | bytes 1540
  158.1 4.3 %copy-start.1 = (f32[254,512]{1,0:T(8,128)S(1)}, f32[254,512]{1,0:T(8,128)}, u32[]{:S(2)}) copy-start(f32[254,512]{1,0:T(8,128)} %slice_bitcast_fusion.1) | copy-start | bytes 1560580
  162.3 3.9 %collective-permute-start.1 = (bf16[256,128]{1,0:T(8,128)(2,1)S(1)}, bf16[256,128]{1,0:T(8,128)(2,1)S(1)}, u32[]{:S(2)}, u32[]{:S(2)}) collective-permute-start(bf16[256,128]{1,0:T(8,128)(2,1)S(1)} %multiply_convert_fusion.7), channel_id=1, source_target_pairs={{0,8},{8,0},{16,24},{24,16},{32,40},{40,32},{48,56},{56,48},{64,72... | collective-permute-start | bytes 196616 | tf_op jit(solution)/shard_map/ppermute | solution.py:26
  164.6 8.0 %copy-start.6 = (f32[2]{0:T(128)S(1)}, f32[2]{0:T(128)}, u32[]{:S(2)}) copy-start(f32[2]{0:T(128)} %copy-done.5) | copy-start | bytes 28
  165.0 8.4 %copy-start.4 = (f32[256,2]{0,1:T(2,128)S(1)}, f32[256,2]{0,1:T(2,128)}, u32[]{:S(2)}) copy-start(f32[256,2]{0,1:T(2,128)} %fusion.56) | copy-start | bytes 6148
  166.3 5.9 %collective-permute-start.2 = (bf16[256,256]{1,0:T(8,128)(2,1)S(1)}, bf16[256,256]{1,0:T(8,128)(2,1)S(1)}, u32[]{:S(2)}, u32[]{:S(2)}) collective-permute-start(bf16[256,256]{1,0:T(8,128)(2,1)S(1)} %maximum_select_fusion.1), channel_id=1, source_target_pairs={{0,16},{16,0},{8,24},{24,8},{32,48},{48,32},{40,56},{56,40},{64,80... | collective-permute-start | bytes 393224 | tf_op jit(solution)/shard_map/ppermute | solution.py:26
  173.6 3.4 %copy-start.20 = (f32[2,8]{1,0:T(2,128)S(1)}, f32[2,8]{1,0:T(2,128)}, u32[]{:S(2)}) copy-start(f32[2,8]{1,0:T(2,128)} %get-tuple-element.40) | copy-start | bytes 196
  174.5 1.2 collective-permute-start.3
  174.6 4.7 %copy-start.19 = (f32[512]{0:T(512)S(1)}, f32[512]{0:T(512)}, u32[]{:S(2)}) copy-start(f32[512]{0:T(512)} %param.29) | copy-start | bytes 6148
  175.7 3.6 %collective-permute-start.4 = (f32[256]{0:T(256)S(1)}, f32[256]{0:T(256)S(1)}, u32[]{:S(2)}, u32[]{:S(2)}) collective-permute-start(f32[256]{0:T(256)S(1)} %add.301), channel_id=1, source_target_pairs={{0,16},{16,0},{8,24},{24,8},{32,48},{48,32},{40,56},{56,40},{64,80... | collective-permute-start | bytes 3080 | tf_op jit(solution)/shard_map/ppermute | solution.py:26
  (10 other events, 19.3 us)

commit v2 on v1

v2 whole, which is shorter than its diff:
```python
import functools

import jax
import jax.numpy as jnp
from jax import lax
from jax.experimental import pallas as pl
from jax.experimental.pallas import tpu as pltpu
from jax.sharding import PartitionSpec as P

HEADS = 256
HEAD_DIM = 64
GROUPS = 8
NORM_EPS = 1e-05
MESH = pl.DeviceIdType.MESH
BF = jnp.bfloat16
F32 = jnp.float32


ORDER = (0, 2, 1, 3)
STEPS = ((0,), (1, 7), (2, 6), (3, 5), (4,))


XC = 640
YC = 512
XR = 656
YR = 192


def project_kernel(
    x_ref, wxz_ref, wbc_ref, wdt_ref, slot_ref, start_ref, prefix_ref, bias_ref, rate_ref, skip_ref,
    cxw_ref, cxb_ref, cbw_ref, cbb_ref, gain_ref, cxp_ref, cbp_ref, pool_hbm,
    y_out, state_out,
    wbd_ref, cbuf, xsb, xst_ref, ybuf, bcg, ssq,
    b_send, b_recv, n_send, n_recv,
    xg, px, px1, px2, pxs, py, py1, py2, pys, sdt, rdt, pool,
    sx, sx1, sx2, sxs, sy, sy1, sy2, sys,
    pool_sem, q_send, q_recv, d_send, d_recv,
    px1_s, px1_r, px2_s, px2_r, py1_s, py1_r, py2_s, py2_r,
    sx1_s, sx1_r, sx2_s, sx2_r, sy1_s, sy1_r, sy2_s, sy2_r,
):
    r = lax.axis_index("req")
    w = lax.axis_index("wide")
    z = w // 4
    j = w % 4

    def wide_at(zz, jj):
        return zz * 4 + jj

    core_w = wide_at(z, j + 1 - 2 * (j % 2))
    side_w = wide_at(z, (j + 2) % 4)
    up_w = wide_at((z + 1) % 8, j)
    down_w = wide_at((z + 7) % 8, j)

    def xor8(a, v):
        out = 0
        for bit in range(3):
            p = 1 << bit
            ab = a // p % 2
            vb = v // p % 2
            out = out + p * ((ab + vb) % 2)
        return out

    pool_copy = pltpu.make_async_copy(pool_hbm, pool, pool_sem)
    pool_copy.start()

    barrier = pltpu.get_barrier_semaphore()
    quad_w = (w, core_w, side_w, wide_at(z, 3 - j))
    for ww in quad_w[1:] + (up_w, down_w):
        pl.semaphore_signal(barrier, inc=1, device_id={"req": r, "wide": ww}, device_id_type=MESH)
    for v in range(1, 8):
        pl.semaphore_signal(
            barrier, inc=1, device_id={"req": xor8(r, v), "wide": w}, device_id_type=MESH
        )
    pl.semaphore_wait(barrier, 12)

    copies = []

    def go(src, dst, ww):
        i = len(copies)
        copy = pltpu.make_async_remote_copy(
            src_ref=src, dst_ref=dst, send_sem=q_send.at[i], recv_sem=q_recv.at[i],
            device_id={"req": r, "wide": ww}, device_id_type=MESH,
        )
        copy.start()
        copies.append(copy)
        return copy

    def plane(src, dst, ssem, rsem, dest):
        return pltpu.make_async_remote_copy(
            src_ref=src, dst_ref=dst, send_sem=ssem, recv_sem=rsem,
            device_id={"req": dest, "wide": w}, device_id_type=MESH,
        )

    side = go(x_ref, xg.at[0, 1], side_w)
    up0 = go(x_ref, xg.at[1, 0], up_w)
    down0 = go(x_ref, xg.at[7, 0], down_w)
    core0 = go(x_ref, xg.at[0, 2], core_w)
    xg[0, 0] = x_ref[...]

    row8x = lax.broadcasted_iota(jnp.int32, (8, 512), 0)
    row8b = lax.broadcasted_iota(jnp.int32, (8, 128), 0)
    cbuf[15:16, :] = jnp.zeros((1, 256), F32)

    def fill_state(v):
        for i in range(2):
            slot = slot_ref[xor8(r, v) * 2 + i]
            mine = slot // 8 == r
            local = jnp.clip(slot - r * 8, 0, 7)
            sx[v, i * 320 : i * 320 + 320] = jnp.where(mine, pool[local, 0:320], 0.0).astype(BF)
            sy[v, i * YR : i * YR + YR] = jnp.where(mine, pool[local, 320:512], 0.0).astype(BF)
            for m in range(3):
                xrow = jnp.sum(jnp.where(row8x == slot - r * 8, cxp_ref[m].astype(F32), 0.0), 0, keepdims=True)
                brow = jnp.sum(jnp.where(row8b == slot - r * 8, cbp_ref[m].astype(F32), 0.0), 0, keepdims=True)
                e = i * 3 + m
                cbuf[2 * e : 2 * e + 1, :] = xrow[:, :256]
                cbuf[2 * e + 1 : 2 * e + 2, :] = xrow[:, 256:]
                cbuf[12 + e // 2 : 13 + e // 2, e % 2 * 128 : e % 2 * 128 + 128] = brow
        sx[v, 640:656] = cbuf[...].astype(BF)

    def sx_first(vy):
        return plane(sx.at[2 * vy + 1], sx1.at[vy], sx1_s.at[vy], sx1_r.at[vy], xor8(r, 1))

    def sy_first(vy):
        return plane(
            sy.at[pl.ds(2 * vy, 2)], sy1.at[vy], sy1_s.at[vy], sy1_r.at[vy], xor8(r, 2 * vy)
        )

    def sx_second(vy):
        return plane(sxs.at[vy], sx2.at[vy], sx2_s.at[vy], sx2_r.at[vy], xor8(r, 2 * vy))

    def sy_second():
        return plane(sys, sy2, sy2_s, sy2_r, xor8(r, 1))

    wbd_ref[:, :128] = wbc_ref[...]
    wide_dt = jnp.concatenate([wdt_ref[...].astype(F32), jnp.zeros((120, 1024), F32)], 0)
    wbd_ref[:, 128:] = wide_dt.T.astype(BF)

    side.wait_recv()
    up1 = go(xg.at[0, 1], xg.at[1, 1], up_w)
    down1 = go(xg.at[0, 1], xg.at[7, 1], down_w)
    core1 = go(xg.at[0, 1], xg.at[0, 3], core_w)
    pool_copy.wait()
    for vy in (1, 3, 2, 0):
        fill_state(2 * vy + 1)
        sx_first(vy).start()
        fill_state(2 * vy)
        if vy:
            sy_first(vy).start()

    rows = [pl.multiple_of(xor8(j, q) * 256, 256) for q in ORDER]

    def compute(k):
        v = (z + 8 - k) % 8
        vy = v // 2
        vh = v % 2
        blocks = [xg[k, p] for p in range(4)]
        for part in range(3):
            def weights(p):
                if part < 2:
                    return wxz_ref[part, pl.ds(rows[p], 256), :]
                return wbd_ref[pl.ds(rows[p], 256), :]

            acc = jnp.dot(blocks[0], weights(0), preferred_element_type=F32)
            for p in range(1, 4):
                acc = acc + jnp.dot(blocks[p], weights(p), preferred_element_type=F32)
            if part == 0:
                py[v] = acc.astype(BF)
            elif part == 1:
                px[v, :, :512] = acc.astype(BF)
            else:
                px[v, :, 512:] = acc[:, :128].astype(BF)
                sdt[v] = acc[:, 128:].T[:8]

        @pl.when(v != 0)
        def _():
            plane(sdt.at[v], rdt.at[v], d_send.at[v], d_recv.at[v], xor8(r, v)).start()

        @pl.when(vh == 1)
        def _():
            plane(px.at[v], px1.at[vy], px1_s.at[vy], px1_r.at[vy], xor8(r, 1)).start()

        @pl.when(vy != 0)
        def _():
            plane(
                py.at[v], py1.at[v], py1_s.at[v], py1_r.at[v], xor8(r, vy * 2)
            ).start()

    def state_second():
        for vy in (1, 3, 2):
            sx_first(vy).wait()
            sxs[vy] = sx[2 * vy] + sx1[vy]
            sx_second(vy).start()
        for vy in (1, 3, 2):
            sy_first(vy).wait()
        sys[...] = (sy[1] + sy1[1, 1]) + (sy1[2, 1] + sy1[3, 1])
        sy_second().start()

    core0.wait_recv()
    core1.wait_recv()
    arrived = {1: (up0, up1), 7: (down0, down1)}
    for step in range(len(STEPS)):
        nxt = STEPS[step + 1] if step + 1 < len(STEPS) else ()
        partner = {}
        later = {}
        for k in nxt:
            for copy in arrived[k]:
                copy.wait_recv()
            partner[k] = go(xg.at[k, 0:2], xg.at[k, 2:4], core_w)
            if k in (1, 2):
                later[k + 1] = (go(xg.at[k, 0:2], xg.at[k + 1, 0:2], up_w),)
            elif k in (7, 6):
                later[k - 1] = (go(xg.at[k, 0:2], xg.at[k - 1, 0:2], down_w),)
            elif k == 3:
                later[4] = later.get(4, ()) + (go(xg.at[3, 0], xg.at[4, 0], up_w),)
            elif k == 5:
                later[4] = later.get(4, ()) + (go(xg.at[5, 1], xg.at[4, 1], down_w),)
        arrived = later
        for k in STEPS[step]:
            compute(k)
        for k in nxt:
            partner[k].wait_recv()

    state_second()

    def px_first(vy):
        return plane(px.at[2 * vy + 1], px1.at[vy], px1_s.at[vy], px1_r.at[vy], xor8(r, 1))

    def py_first(v):
        return plane(py.at[v], py1.at[v], py1_s.at[v], py1_r.at[v], xor8(r, v // 2 * 2))

    def px_second(vy):
        return plane(pxs.at[vy], px2.at[vy], px2_s.at[vy], px2_r.at[vy], xor8(r, 2 * vy))

    def py_second():
        return plane(pys, py2, py2_s, py2_r, xor8(r, 1))

    for vy in (1, 3, 2):
        px_first(vy).wait()
        pxs[vy] = (px[2 * vy].astype(F32) + px1[vy].astype(F32)).astype(BF)
        px_second(vy).start()
    for v in (3, 5, 7):
        py_first(v).wait()
    pys[...] = (
        (py[1].astype(F32) + py1[3].astype(F32)) + (py1[5].astype(F32) + py1[7].astype(F32))
    ).astype(BF)
    py_second().start()

    for copy in copies:
        copy.wait_send()
    for v in (2, 4, 6):
        py_first(v).wait()
    for v in range(1, 8):
        plane(sdt.at[v], rdt.at[v], d_send.at[v], d_recv.at[v], xor8(r, v)).wait()
    dts = sdt[0]
    for v in range(1, 8):
        dts = dts + rdt[v]
    px_first(0).wait()
    sx_first(0).wait()
    for vy in (1, 3, 2):
        sx_second(vy).wait()
        px_second(vy).wait()
    cbuf[...] = (
        (sx[0, 640:656] + sx1[0, 640:656]) + (sx2[1, 640:656] + sx2[2, 640:656]) + sx2[3, 640:656]
    ).astype(F32)

    start = start_ref[0, 1]
    live = [jnp.where(prefix_ref[i] > 0, 1.0, 0.0) for i in range(2)]

    def total_x(c0, n):
        cols = slice(c0, c0 + n)
        out = px[0, :, cols].astype(F32) + px1[0, :, cols].astype(F32)
        for vy in (1, 2, 3):
            out = out + px2[vy, :, cols].astype(F32)
        return out.astype(BF).astype(F32)

    def conv(values, taps, bias, cache):
        n = values.shape[1]
        tok = lax.broadcasted_iota(jnp.int32, (256, n), 0)
        out = bias + taps[3:4] * values
        for lag in range(1, 4):
            earlier = pltpu.roll(values, lag, 0)
            for i in range(2):
                for o in range(lag):
                    at = o if i == 0 else start + o
                    earlier = jnp.where(tok == at, cache(i, 3 + o - lag), earlier)
            out = out + taps[3 - lag : 4 - lag] * earlier
        return jax.nn.silu(out).astype(BF)

    def cache_b(i, m):
        e = i * 3 + m
        return cbuf[12 + e // 2 : 13 + e // 2, e % 2 * 128 : e % 2 * 128 + 128] * live[i]

    bcg[0] = conv(total_x(512, 128), cbw_ref[...], cbb_ref[...], cache_b)
    shares = []
    for q in range(1, 4):
        copy = pltpu.make_async_remote_copy(
            src_ref=bcg.at[0], dst_ref=bcg.at[q], send_sem=b_send.at[q], recv_sem=b_recv.at[q],
            device_id={"req": r, "wide": quad_w[q]}, device_id_type=MESH,
        )
        copy.start()
        shares.append(copy)

    for half in range(2):
        def cache_x(i, m):
            e = 2 * (i * 3 + m) + half
            return cbuf[e : e + 1, :] * live[i]

        cols = slice(half * 256, half * 256 + 256)
        xs = conv(total_x(half * 256, 256), cxw_ref[:, cols], cxb_ref[:, cols], cache_x)
        xsb[:, cols] = xs
        xst_ref[cols, :] = xs.astype(F32).T

    head = lax.broadcasted_iota(jnp.int32, (8, 256), 0)
    lane = lax.broadcasted_iota(jnp.int32, (8, 256), 1)
    bias8 = jnp.zeros((8, 256), F32)
    rate8 = jnp.zeros((8, 256), F32)
    for h in range(8):
        bias8 = jnp.where(head == h, bias_ref[h], bias8)
        rate8 = jnp.where(head == h, rate_ref[h], rate8)
    raised = dts.astype(BF).astype(F32) + bias8
    step = jnp.maximum(raised, 0.0) + jnp.log1p(jnp.exp(-jnp.abs(raised)))
    rate = -jnp.exp(rate8) * step
    upper_s = lax.broadcasted_iota(jnp.int32, (256, 256), 0)
    upper_t = lax.broadcasted_iota(jnp.int32, (256, 256), 1)
    reach = jnp.where((upper_s <= upper_t) & ((upper_t < start) | (upper_s >= start)), 1.0, 0.0)
    top = rate.astype(BF).astype(F32)
    mid = (rate - top).astype(BF).astype(F32)
    low = rate - top - mid
    parts = jnp.concatenate([top, mid, low, jnp.zeros((8, 256), F32)], 0).astype(BF)
    sums = jnp.dot(parts, reach.astype(BF), preferred_element_type=F32)
    run = sums[0:8] + sums[8:16] + sums[16:24]
    late = lane >= start
    end = [
        jnp.sum(jnp.where(late, 0.0, rate), 1, keepdims=True),
        jnp.sum(jnp.where(late, rate, 0.0), 1, keepdims=True),
    ]
    to_end = jnp.exp(jnp.where(late, end[1], end[0]) - run) * step
    end_decay = [jnp.exp(end[0]), jnp.exp(end[1])]
    columns = jnp.concatenate([run, jnp.exp(run), jnp.zeros((112, 256), F32)], 0).T

    for copy in shares:
        copy.wait()

    def maps(a):
        ab = (a % 2 + j % 2) % 2 + 2 * ((a // 2 + j // 2) % 2)
        return bcg[ab]

    b_maps = jnp.concatenate([maps(0), maps(1)], 1)
    c_maps = jnp.concatenate([maps(2), maps(3)], 1)
    scores = lax.dot_general(
        c_maps, b_maps, (((1,), (1,)), ((), ())), preferred_element_type=F32
    )
    allowed = (upper_t <= upper_s) & ((upper_s < start) | (upper_t >= start))
    scores = jnp.where(allowed, scores, 0.0)
    first = lax.broadcasted_iota(jnp.int32, (256, 128), 1) < 64
    for pair in range(4):
        cols = slice(pair * 128, pair * 128 + 128)
        xs = xsb[:, cols]
        acc = None
        for side_h in range(2):
            h = 2 * pair + side_h
            gap = jnp.minimum(columns[:, h : h + 1] - run[h : h + 1, :], 0.0)
            weight = (jnp.exp(gap) * step[h : h + 1, :] * scores).astype(BF)
            kept = jnp.where(first == (side_h == 0), xs.astype(F32), 0.0).astype(BF)
            part = jnp.dot(weight, kept, preferred_element_type=F32)
            acc = part if acc is None else acc + part
        skip = jnp.where(first, skip_ref[2 * pair], skip_ref[2 * pair + 1])
        ybuf[:, cols] = acc + skip * xs.astype(F32)

    sy_second().wait()
    py_second().wait()

    def h0_piece(i, h):
        if h < 5:
            rows_h = slice(i * 320 + h * 64, i * 320 + h * 64 + 64)
            return (sx[0, rows_h] + sx1[0, rows_h]) + (sx2[1, rows_h] + sx2[2, rows_h]) + sx2[3, rows_h]
        rows_h = slice(i * YR + (h - 5) * 64, i * YR + (h - 5) * 64 + 64)
        return (
            (sy[0, rows_h] + sy1[1, 0, rows_h]) + (sy1[2, 0, rows_h] + sy1[3, 0, rows_h]) + sy2[rows_h]
        )

    square = jnp.zeros((256, 128), F32)
    tok = lax.broadcasted_iota(jnp.int32, (256, 128), 0)
    h0 = [[None] * 8, [None] * 8]
    for pair in range(4):
        cols = slice(pair * 128, pair * 128 + 128)
        from_state = None
        for i in range(2):
            for h in (2 * pair, 2 * pair + 1):
                h0[i][h] = h0_piece(i, h)
            both = jnp.concatenate([h0[i][2 * pair], h0[i][2 * pair + 1]], 0)
            part = lax.dot_general(
                c_maps, both, (((1,), (1,)), ((), ())), preferred_element_type=F32
            ) * live[i]
            from_state = part if i == 0 else jnp.where(tok >= start, part, from_state)
        grown = jnp.where(
            first, columns[:, 8 + 2 * pair : 9 + 2 * pair], columns[:, 9 + 2 * pair : 10 + 2 * pair]
        )
        result = ybuf[:, cols] + from_state * grown
        gate = py[0, :, cols].astype(F32) + py2[:, cols].astype(F32)
        for v in (2, 4, 6):
            gate = gate + py1[v, :, cols].astype(F32)
        gated = result * jax.nn.silu(gate.astype(BF).astype(F32))
        ybuf[:, cols] = gated
        square = square + gated * gated

    ssq[0] = jnp.broadcast_to(jnp.sum(square.T, 0, keepdims=True), (8, 256))
    norms = []
    for q in range(1, 4):
        copy = pltpu.make_async_remote_copy(
            src_ref=ssq.at[0], dst_ref=ssq.at[q], send_sem=n_send.at[q], recv_sem=n_recv.at[q],
            device_id={"req": r, "wide": quad_w[q]}, device_id_type=MESH,
        )
        copy.start()
        norms.append(copy)

    for h in range(8):
        rows_h = slice(h * 64, h * 64 + 64)
        spread = xst_ref[rows_h, :] * to_end[h : h + 1, :]
        late_row = lax.broadcasted_iota(jnp.int32, (64, 256), 1) >= start
        for i in range(2):
            u = jnp.where(late_row == (i == 1), spread, 0.0).astype(BF)
            fresh = jnp.dot(u, b_maps, preferred_element_type=F32)
            keep = end_decay[i][h : h + 1, :] * live[i]
            state_out[i, rows_h, :] = keep * h0[i][h].astype(F32) + fresh

    for copy in norms:
        copy.wait()
    mean = (ssq[0] + ssq[1] + ssq[2] + ssq[3]) / (HEADS * HEAD_DIM // GROUPS)
    scale = jnp.broadcast_to(lax.rsqrt(mean + NORM_EPS)[0:1], (128, 256)).T
    for pair in range(4):
        cols = slice(pair * 128, pair * 128 + 128)
        y_out[:, cols] = (ybuf[:, cols] * scale * gain_ref[:, cols]).astype(BF)


def project(*args):
    vm = pl.BlockSpec(memory_space=pltpu.VMEM)
    sm = pl.BlockSpec(memory_space=pltpu.SMEM)
    dma = pltpu.SemaphoreType.DMA
    n_q = 7 + 7 + 6
    return pl.pallas_call(
        project_kernel,
        out_shape=(
            jax.ShapeDtypeStruct((256, 512), BF),
            jax.ShapeDtypeStruct((2, 512, 256), F32),
        ),
        in_specs=[vm] * 4 + [sm] * 6 + [vm] * 7 + [pl.BlockSpec(memory_space=pl.ANY)],
        out_specs=(vm,) * 2,
        scratch_shapes=[
            pltpu.VMEM((1024, 256), BF),
            pltpu.VMEM((16, 256), F32),
            pltpu.VMEM((256, 512), BF),
            pltpu.VMEM((512, 256), F32),
            pltpu.VMEM((256, 512), F32),
            pltpu.VMEM((4, 256, 128), BF),
            pltpu.VMEM((4, 8, 256), F32),
            dma((4,)), dma((4,)), dma((4,)), dma((4,)),
            pltpu.VMEM((8, 4, 256, 256), BF),
            pltpu.VMEM((8, 256, XC), BF),
            pltpu.VMEM((4, 256, XC), BF),
            pltpu.VMEM((4, 256, XC), BF),
            pltpu.VMEM((4, 256, XC), BF),
            pltpu.VMEM((8, 256, YC), BF),
            pltpu.VMEM((8, 256, YC), BF),
            pltpu.VMEM((256, YC), BF),
            pltpu.VMEM((256, YC), BF),
            pltpu.VMEM((8, 8, 256), F32),
            pltpu.VMEM((8, 8, 256), F32),
            pltpu.VMEM((8, 512, 256), F32),
            pltpu.VMEM((8, XR, 256), BF),
            pltpu.VMEM((4, XR, 256), BF),
            pltpu.VMEM((4, XR, 256), BF),
            pltpu.VMEM((4, XR, 256), BF),
            pltpu.VMEM((8, 2 * YR, 256), BF),
            pltpu.VMEM((4, 2, 2 * YR, 256), BF),
            pltpu.VMEM((2 * YR, 256), BF),
            pltpu.VMEM((2 * YR, 256), BF),
            dma(()),
            dma((n_q,)), dma((n_q,)), dma((8,)), dma((8,)),
            dma((4,)), dma((4,)), dma((4,)), dma((4,)), dma((8,)), dma((8,)), dma(()), dma(()),
            dma((4,)), dma((4,)), dma((4,)), dma((4,)), dma((4,)), dma((4,)), dma(()), dma(()),
        ],
        compiler_params=pltpu.CompilerParams(
            collective_id=0, has_side_effects=True, vmem_limit_bytes=56 << 20
        ),
        name="project",
    )(*args)


def on_device(
    x_in, w_xz, w_dt, w_bc, dt_bias, a_log, d_skip, conv_x_w, conv_x_b, conv_bc_w, conv_bc_b,
    norm_gain, stretch_start, prefix_len, state_slot, ssm_pool, conv_x_pool, conv_bc_pool,
):
    route = []
    for r in range(8):
        for w in range(32):
            f, j = w // 4, w % 4
            route.append((w * 8 + r, ((r ^ f) * 4 + j) * 8 + f))
    x_t = lax.ppermute(x_in, ("wide", "req"), route)
    y, state = project(
        x_t, jnp.transpose(w_xz, (1, 0, 2)), w_bc, w_dt.T,
        state_slot, stretch_start, prefix_len, dt_bias, a_log, d_skip,
        conv_x_w, conv_x_b[None], conv_bc_w, conv_bc_b[None], norm_gain[None],
        jnp.transpose(conv_x_pool, (1, 0, 2)), jnp.transpose(conv_bc_pool, (1, 0, 2)),
        ssm_pool.reshape(8, 512, 256),
    )
    return y, state.reshape(2, 8, 64, 256)


def solution(mesh):
    in_specs = (
        P("req", "wide"), P("req", None, "wide"), P("req", "wide"), P("req", "wide"),
        P("wide"), P("wide"), P("wide"), P(None, "wide"), P("wide"), P(None, "wide"),
        P("wide"), P("wide"), P("req", None), P("req"), P(),
        P("req", "wide", None, None), P("req", None, "wide"), P("req", None, "wide"),
    )
    out_specs = (P("req", "wide"), P("req", "wide", None, None))
    return jax.shard_map(
        on_device, mesh=mesh, in_specs=in_specs, out_specs=out_specs, check_vma=False
    )
```

time: 181 us -> 121 us (0.67)
  the two profiles are of different devices: /device:TPU:240 before, /device:TPU:1 now
where the time goes in v2:
time: 121 us
  Pallas kernels  110 us (91%)
  local copies, waits for them, and re-layouts  7.88 us (7%)
  starting transfers between devices  1.56 us (1%)
    pallas_call x1, Pallas kernels, project(): pl.pallas_call(project_kernel, out_shape=(jax.ShapeDtypeStruct((256, 512)...  110 us
    unnamed x5, local copies, waits for them, and re-layouts  7.88 us
  transfers between devices with their start and end apart: 1, of which 0 were waited for; matrix products, arithmetic and copies ran while one was open for 3% of the time, Pallas kernels for 0%

profile of v2, /device:TPU:1, one launch (start us, length us, event | category | flops | bytes accessed | tf_op | source)
XLA Modules:
  0.0 120.6 jit_solution(4103685527838253675)
XLA Ops:
  0.6 1.6 %collective-permute-start = (bf16[256,256]{1,0:T(8,128)(2,1)}, bf16[256,256]{1,0:T(8,128)(2,1)S(1)}, u32[]{:S(2)}, u32[]{:S(2)}) collective-permute-start(bf16[256,256]{1,0:T(8,128)(2,1)} %param.18), channel_id=1, source_target_pairs={{0,0},{8,8},{16,16},{24,24},{32,33},{40,41},{48,49},{56,57},{64,66... | collective-permute-start | bytes 393224 | tf_op jit(solution)/shard_map/ppermute | solution.py:499
  2.2 3.3 %copy.22 = bf16[1024,2,512]{2,0,1:T(8,128)(2,1)} copy(bf16[1024,2,512]{2,1,0:T(2,128)(2,1)} %param.19) | data formatting | bytes 4194304 | tf_op args[1]
  5.5 0.0 collective-permute-done.x_ref
  5.5 0.0 copy-start
  5.5 0.7 copy-done
  6.1 110.5 %project.1 = (bf16[256,512]{1,0:T(8,128)(2,1)}, f32[2,512,256]{2,1,0:T(8,128)}) custom-call(bf16[256,256]{1,0:T(8,128)(2,1)} %copy-done, bf16[2,1024,512]{2,1,0:T(8,128)(2,1)} %bitcast.11, bf16[1024,128]{1,0:T(8,128)(2,1)} %wbc_ref.1, bf16[8,1024]{1,0:T(8,128)(2,1)} %bitcast.15, s32[16]{0:T(128)} %slot_ref.1, s32[1,2]{1,0:T(1,128)} %start_ref.1, ...), custom_call_target="tpu_custom_call" | custom-call | tf_op jit(solution)/shard_map/project/pallas_call | solution.py:441
  116.6 1.7 %copy.25 = bf16[256,512]{1,0:T(8,128)(2,1)} copy(bf16[256,512]{1,0:T(8,128)(2,1)} %get-tuple-element.8) | data formatting | bytes 524288
  118.3 2.3 %copy.26 = f32[2,8,64,256]{3,2,1,0:T(8,128)} copy(f32[2,8,64,256]{3,2,1,0:T(8,128)} %bitcast.13) | data formatting | bytes 2097152
Async XLA Ops:
  0.6 4.8 %collective-permute-start = (bf16[256,256]{1,0:T(8,128)(2,1)}, bf16[256,256]{1,0:T(8,128)(2,1)S(1)}, u32[]{:S(2)}, u32[]{:S(2)}) collective-permute-start(bf16[256,256]{1,0:T(8,128)(2,1)} %param.18), channel_id=1, source_target_pairs={{0,0},{8,8},{16,16},{24,24},{32,33},{40,41},{48,49},{56,57},{64,66... | collective-permute-start | bytes 393224 | tf_op jit(solution)/shard_map/ppermute | solution.py:499
  5.5 0.7 copy-start

commit v3 on v2

--- a/solution.py
+++ b/solution.py
@@ -22,8 +22,9 @@
 
 XC = 640
 YC = 512
-XR = 656
-YR = 192
+XR = 400
+YR = 320
+CUT = 208
 
 
 def project_kernel(
@@ -31,7 +32,7 @@
     cxw_ref, cxb_ref, cbw_ref, cbb_ref, gain_ref, cxp_ref, cbp_ref, pool_hbm,
     y_out, state_out,
     wbd_ref, cbuf, xsb, xst_ref, ybuf, bcg, ssq,
-    b_send, b_recv, n_send, n_recv,
+    b_send, b_recv, n_send, n_recv, via_sy, via_sx, via_px, via_s, via_r,
     xg, px, px1, px2, pxs, py, py1, py2, pys, sdt, rdt, pool,
     sx, sx1, sx2, sxs, sy, sy1, sy2, sys,
     pool_sem, q_send, q_recv, d_send, d_recv,
@@ -106,8 +107,8 @@
             slot = slot_ref[xor8(r, v) * 2 + i]
             mine = slot // 8 == r
             local = jnp.clip(slot - r * 8, 0, 7)
-            sx[v, i * 320 : i * 320 + 320] = jnp.where(mine, pool[local, 0:320], 0.0).astype(BF)
-            sy[v, i * YR : i * YR + YR] = jnp.where(mine, pool[local, 320:512], 0.0).astype(BF)
+            sx[v, i * 192 : i * 192 + 192] = jnp.where(mine, pool[local, 0:192], 0.0).astype(BF)
+            sy[v, i * YR : i * YR + YR] = jnp.where(mine, pool[local, 192:512], 0.0).astype(BF)
             for m in range(3):
                 xrow = jnp.sum(jnp.where(row8x == slot - r * 8, cxp_ref[m].astype(F32), 0.0), 0, keepdims=True)
                 brow = jnp.sum(jnp.where(row8b == slot - r * 8, cbp_ref[m].astype(F32), 0.0), 0, keepdims=True)
@@ -115,7 +116,7 @@
                 cbuf[2 * e : 2 * e + 1, :] = xrow[:, :256]
                 cbuf[2 * e + 1 : 2 * e + 2, :] = xrow[:, 256:]
                 cbuf[12 + e // 2 : 13 + e // 2, e % 2 * 128 : e % 2 * 128 + 128] = brow
-        sx[v, 640:656] = cbuf[...].astype(BF)
+        sx[v, 384:400] = cbuf[...].astype(BF)
 
     def sx_first(vy):
         return plane(sx.at[2 * vy + 1], sx1.at[vy], sx1_s.at[vy], sx1_r.at[vy], xor8(r, 1))
@@ -140,11 +141,24 @@
     down1 = go(xg.at[0, 1], xg.at[7, 1], down_w)
     core1 = go(xg.at[0, 1], xg.at[0, 3], core_w)
     pool_copy.wait()
-    for vy in (1, 3, 2, 0):
+    def via(n, src, dst):
+        return plane(src, dst, via_s.at[n], via_r.at[n], xor8(r, 2 + 4 * (n % 2)))
+
+    def sy_via(n):
+        return via(n, sy.at[4 + n], via_sy.at[n])
+
+    for vy in (2, 1, 3, 0):
+        fill_state(2 * vy)
         fill_state(2 * vy + 1)
+        if vy == 2:
+            sy_via(0).start()
+            sy_via(1).start()
         sx_first(vy).start()
-        fill_state(2 * vy)
-        if vy:
+
+    def state_join():
+        for n, own, vy in ((0, 6, 3), (1, 3, 1)):
+            sy_via(n).wait()
+            sy[own] = sy[own] + via_sy[n]
             sy_first(vy).start()
 
     rows = [pl.multiple_of(xor8(j, q) * 256, 256) for q in ORDER]
@@ -185,15 +199,30 @@
                 py.at[v], py1.at[v], py1_s.at[v], py1_r.at[v], xor8(r, vy * 2)
             ).start()
 
+    def sx_via(n):
+        part = slice(0, CUT) if n == 0 else slice(CUT, XR)
+        return via(2 + n, sxs.at[2, part], via_sx.at[part])
+
     def state_second():
-        for vy in (1, 3, 2):
+        sx_first(2).wait()
+        sxs[2] = sx[4] + sx1[2]
+        sx_via(0).start()
+        sx_via(1).start()
+        for vy in (1, 3):
             sx_first(vy).wait()
             sxs[vy] = sx[2 * vy] + sx1[vy]
-            sx_second(vy).start()
-        for vy in (1, 3, 2):
+        for vy in (1, 3):
             sy_first(vy).wait()
-        sys[...] = (sy[1] + sy1[1, 1]) + (sy1[2, 1] + sy1[3, 1])
+        sys[...] = (sy[1] + sy1[1, 1]) + sy1[3, 1]
         sy_second().start()
+
+    def state_third():
+        sx_via(0).wait()
+        sxs[3, :CUT] = sxs[3, :CUT] + via_sx[:CUT]
+        sx_second(3).start()
+        sx_via(1).wait()
+        sxs[1, CUT:] = sxs[1, CUT:] + via_sx[CUT:]
+        sx_second(1).start()
 
     core0.wait_recv()
     core1.wait_recv()
@@ -217,6 +246,8 @@
         arrived = later
         for k in STEPS[step]:
             compute(k)
+        if step == 0:
+            state_join()
         for k in nxt:
             partner[k].wait_recv()
 
@@ -234,9 +265,23 @@
     def py_second():
         return plane(pys, py2, py2_s, py2_r, xor8(r, 1))
 
-    for vy in (1, 3, 2):
+    def px_via(n):
+        part = slice(128 * n, 128 * n + 128)
+        return via(4 + n, pxs.at[2, part], via_px.at[part])
+
+    px_first(2).wait()
+    pxs[2] = (px[4].astype(F32) + px1[2].astype(F32)).astype(BF)
+    px_via(0).start()
+    px_via(1).start()
+    state_third()
+    for n, vy in ((0, 3), (1, 1)):
         px_first(vy).wait()
-        pxs[vy] = (px[2 * vy].astype(F32) + px1[vy].astype(F32)).astype(BF)
+        px_via(n).wait()
+        part = slice(128 * n, 128 * n + 128)
+        rest = slice(128 - 128 * n, 256 - 128 * n)
+        joined = px[2 * vy, part].astype(F32) + px1[vy, part].astype(F32) + via_px[part].astype(F32)
+        pxs[vy, part] = joined.astype(BF)
+        pxs[vy, rest] = (px[2 * vy, rest].astype(F32) + px1[vy, rest].astype(F32)).astype(BF)
         px_second(vy).start()
     for v in (3, 5, 7):
         py_first(v).wait()
@@ -256,11 +301,11 @@
         dts = dts + rdt[v]
     px_first(0).wait()
     sx_first(0).wait()
-    for vy in (1, 3, 2):
+    for vy in (1, 3):
         sx_second(vy).wait()
         px_second(vy).wait()
     cbuf[...] = (
-        (sx[0, 640:656] + sx1[0, 640:656]) + (sx2[1, 640:656] + sx2[2, 640:656]) + sx2[3, 640:656]
+        (sx[0, 384:400] + sx1[0, 384:400]) + (sx2[1, 384:400] + sx2[3, 384:400])
     ).astype(F32)
 
     start = start_ref[0, 1]
@@ -269,7 +314,7 @@
     def total_x(c0, n):
         cols = slice(c0, c0 + n)
         out = px[0, :, cols].astype(F32) + px1[0, :, cols].astype(F32)
-        for vy in (1, 2, 3):
+        for vy in (1, 3):
             out = out + px2[vy, :, cols].astype(F32)
         return out.astype(BF).astype(F32)
 
@@ -371,12 +416,12 @@
     py_second().wait()
 
     def h0_piece(i, h):
-        if h < 5:
-            rows_h = slice(i * 320 + h * 64, i * 320 + h * 64 + 64)
-            return (sx[0, rows_h] + sx1[0, rows_h]) + (sx2[1, rows_h] + sx2[2, rows_h]) + sx2[3, rows_h]
-        rows_h = slice(i * YR + (h - 5) * 64, i * YR + (h - 5) * 64 + 64)
+        if h < 3:
+            rows_h = slice(i * 192 + h * 64, i * 192 + h * 64 + 64)
+            return (sx[0, rows_h] + sx1[0, rows_h]) + (sx2[1, rows_h] + sx2[3, rows_h])
+        rows_h = slice(i * YR + (h - 3) * 64, i * YR + (h - 3) * 64 + 64)
         return (
-            (sy[0, rows_h] + sy1[1, 0, rows_h]) + (sy1[2, 0, rows_h] + sy1[3, 0, rows_h]) + sy2[rows_h]
+            (sy[0, rows_h] + sy1[1, 0, rows_h]) + (sy1[3, 0, rows_h] + sy2[rows_h])
         )
 
     square = jnp.zeros((256, 128), F32)
@@ -455,6 +500,10 @@
             pltpu.VMEM((4, 256, 128), BF),
             pltpu.VMEM((4, 8, 256), F32),
             dma((4,)), dma((4,)), dma((4,)), dma((4,)),
+            pltpu.VMEM((2, 2 * YR, 256), BF),
+            pltpu.VMEM((XR, 256), BF),
+            pltpu.VMEM((256, XC), BF),
+            dma((6,)), dma((6,)),
             pltpu.VMEM((8, 4, 256, 256), BF),
             pltpu.VMEM((8, 256, XC), BF),
             pltpu.VMEM((4, 256, XC), BF),

time: 121 us -> 113 us (0.934)
  the two profiles are of different devices: /device:TPU:1 before, /device:TPU:101 now
where the time goes in v3:
time: 113 us; the launch traced here: 112 us
  Pallas kernels  96.3 us (85%)
  local copies, waits for them, and re-layouts  7.88 us (7%)
  waiting for transfers between devices  4.67 us (4%)
  starting transfers between devices  2.75 us (2%)
    pallas_call x1, Pallas kernels, project(): pl.pallas_call(project_kernel, out_shape=(jax.ShapeDtypeStruct((256, 512)...  96.3 us
    unnamed x5, local copies, waits for them, and re-layouts  7.88 us
    ppermute x1, waiting for transfers between devices, on_device(): x_t = lax.ppermute(x_in, ('wide', 'req'), route)  4.67 us
    ppermute x1, starting transfers between devices, on_device(): x_t = lax.ppermute(x_in, ('wide', 'req'), route)  2.75 us
  transfers between devices with their start and end apart: 1, of which 1 were waited for; matrix products, arithmetic and copies ran while one was open for 3% of the time, Pallas kernels for 0%

profile of v3, /device:TPU:101, one launch (start us, length us, event | category | flops | bytes accessed | tf_op | source)
XLA Modules:
  0.0 112.3 jit_solution(16202209627018385599)
XLA Ops:
  0.6 2.7 %collective-permute-start = (bf16[256,256]{1,0:T(8,128)(2,1)}, bf16[256,256]{1,0:T(8,128)(2,1)S(1)}, u32[]{:S(2)}, u32[]{:S(2)}) collective-permute-start(bf16[256,256]{1,0:T(8,128)(2,1)} %param.18), channel_id=1, source_target_pairs={{0,0},{8,8},{16,16},{24,24},{32,33},{40,41},{48,49},{56,57},{64,66... | collective-permute-start | bytes 393224 | tf_op jit(solution)/shard_map/ppermute | solution.py:548
  3.4 3.3 %copy.22 = bf16[1024,2,512]{2,0,1:T(8,128)(2,1)} copy(bf16[1024,2,512]{2,1,0:T(2,128)(2,1)} %param.19) | data formatting | bytes 4194304 | tf_op args[1]
  6.6 4.7 %collective-permute-done.x_ref = bf16[256,256]{1,0:T(8,128)(2,1)S(1)} collective-permute-done((bf16[256,256]{1,0:T(8,128)(2,1)}, bf16[256,256]{1,0:T(8,128)(2,1)S(1)}, u32[]{:S(2)}, u32[]{:S(2)}) %collective-permute-start) | collective-permute-done | bytes 131104 | tf_op jit(solution)/shard_map/ppermute | solution.py:548
  11.3 0.0 copy-start
  11.3 0.7 copy-done
  12.0 96.3 %project.1 = (bf16[256,512]{1,0:T(8,128)(2,1)}, f32[2,512,256]{2,1,0:T(8,128)}) custom-call(bf16[256,256]{1,0:T(8,128)(2,1)} %copy-done, bf16[2,1024,512]{2,1,0:T(8,128)(2,1)} %bitcast.11, bf16[1024,128]{1,0:T(8,128)(2,1)} %wbc_ref.1, bf16[8,1024]{1,0:T(8,128)(2,1)} %bitcast.15, s32[16]{0:T(128)} %slot_ref.1, s32[1,2]{1,0:T(1,128)} %start_ref.1, ...), custom_call_target="tpu_custom_call" | custom-call | tf_op jit(solution)/shard_map/project/pallas_call | solution.py:486
  108.3 1.7 %copy.25 = bf16[256,512]{1,0:T(8,128)(2,1)} copy(bf16[256,512]{1,0:T(8,128)(2,1)} %get-tuple-element.8) | data formatting | bytes 524288
  110.0 2.3 %copy.26 = f32[2,8,64,256]{3,2,1,0:T(8,128)} copy(f32[2,8,64,256]{3,2,1,0:T(8,128)} %bitcast.13) | data formatting | bytes 2097152
Async XLA Ops:
  0.6 10.7 %collective-permute-start = (bf16[256,256]{1,0:T(8,128)(2,1)}, bf16[256,256]{1,0:T(8,128)(2,1)S(1)}, u32[]{:S(2)}, u32[]{:S(2)}) collective-permute-start(bf16[256,256]{1,0:T(8,128)(2,1)} %param.18), channel_id=1, source_target_pairs={{0,0},{8,8},{16,16},{24,24},{32,33},{40,41},{48,49},{56,57},{64,66... | collective-permute-start | bytes 393224 | tf_op jit(solution)/shard_map/ppermute | solution.py:548
  11.3 0.7 copy-start

commit v4 on v3

--- a/solution.py
+++ b/solution.py
@@ -226,30 +226,33 @@
 
     core0.wait_recv()
     core1.wait_recv()
-    arrived = {1: (up0, up1), 7: (down0, down1)}
+    arrived = {(1, 0): up0, (1, 1): up1, (7, 0): down0, (7, 1): down1}
     for step in range(len(STEPS)):
         nxt = STEPS[step + 1] if step + 1 < len(STEPS) else ()
-        partner = {}
-        later = {}
-        for k in nxt:
-            for copy in arrived[k]:
+        partner = []
+
+        def forward(p):
+            for k in nxt:
+                copy = arrived.pop((k, p), None)
+                if copy is None:
+                    continue
                 copy.wait_recv()
-            partner[k] = go(xg.at[k, 0:2], xg.at[k, 2:4], core_w)
-            if k in (1, 2):
-                later[k + 1] = (go(xg.at[k, 0:2], xg.at[k + 1, 0:2], up_w),)
-            elif k in (7, 6):
-                later[k - 1] = (go(xg.at[k, 0:2], xg.at[k - 1, 0:2], down_w),)
-            elif k == 3:
-                later[4] = later.get(4, ()) + (go(xg.at[3, 0], xg.at[4, 0], up_w),)
-            elif k == 5:
-                later[4] = later.get(4, ()) + (go(xg.at[5, 1], xg.at[4, 1], down_w),)
-        arrived = later
-        for k in STEPS[step]:
+                block = xg.at[k, p]
+                if k in (1, 2) or (k == 3 and p == 0):
+                    arrived[k + 1, p] = go(block, xg.at[k + 1, p], up_w)
+                elif k in (7, 6) or (k == 5 and p == 1):
+                    arrived[k - 1, p] = go(block, xg.at[k - 1, p], down_w)
+                partner.append(go(block, xg.at[k, p + 2], core_w))
+
+        forward(0)
+        compute(STEPS[step][0])
+        forward(1)
+        for k in STEPS[step][1:]:
             compute(k)
         if step == 0:
             state_join()
-        for k in nxt:
-            partner[k].wait_recv()
+        for copy in partner:
+            copy.wait_recv()
 
     state_second()
 
@@ -299,61 +302,9 @@
     dts = sdt[0]
     for v in range(1, 8):
         dts = dts + rdt[v]
-    px_first(0).wait()
-    sx_first(0).wait()
-    for vy in (1, 3):
-        sx_second(vy).wait()
-        px_second(vy).wait()
-    cbuf[...] = (
-        (sx[0, 384:400] + sx1[0, 384:400]) + (sx2[1, 384:400] + sx2[3, 384:400])
-    ).astype(F32)
 
     start = start_ref[0, 1]
     live = [jnp.where(prefix_ref[i] > 0, 1.0, 0.0) for i in range(2)]
-
-    def total_x(c0, n):
-        cols = slice(c0, c0 + n)
-        out = px[0, :, cols].astype(F32) + px1[0, :, cols].astype(F32)
-        for vy in (1, 3):
-            out = out + px2[vy, :, cols].astype(F32)
-        return out.astype(BF).astype(F32)
-
-    def conv(values, taps, bias, cache):
-        n = values.shape[1]
-        tok = lax.broadcasted_iota(jnp.int32, (256, n), 0)
-        out = bias + taps[3:4] * values
-        for lag in range(1, 4):
-            earlier = pltpu.roll(values, lag, 0)
-            for i in range(2):
-                for o in range(lag):
-                    at = o if i == 0 else start + o
-                    earlier = jnp.where(tok == at, cache(i, 3 + o - lag), earlier)
-            out = out + taps[3 - lag : 4 - lag] * earlier
-        return jax.nn.silu(out).astype(BF)
-
-    def cache_b(i, m):
-        e = i * 3 + m
-        return cbuf[12 + e // 2 : 13 + e // 2, e % 2 * 128 : e % 2 * 128 + 128] * live[i]
-
-    bcg[0] = conv(total_x(512, 128), cbw_ref[...], cbb_ref[...], cache_b)
-    shares = []
-    for q in range(1, 4):
-        copy = pltpu.make_async_remote_copy(
-            src_ref=bcg.at[0], dst_ref=bcg.at[q], send_sem=b_send.at[q], recv_sem=b_recv.at[q],
-            device_id={"req": r, "wide": quad_w[q]}, device_id_type=MESH,
-        )
-        copy.start()
-        shares.append(copy)
-
-    for half in range(2):
-        def cache_x(i, m):
-            e = 2 * (i * 3 + m) + half
-            return cbuf[e : e + 1, :] * live[i]
-
-        cols = slice(half * 256, half * 256 + 256)
-        xs = conv(total_x(half * 256, 256), cxw_ref[:, cols], cxb_ref[:, cols], cache_x)
-        xsb[:, cols] = xs
-        xst_ref[cols, :] = xs.astype(F32).T
 
     head = lax.broadcasted_iota(jnp.int32, (8, 256), 0)
     lane = lax.broadcasted_iota(jnp.int32, (8, 256), 1)
@@ -383,6 +334,59 @@
     end_decay = [jnp.exp(end[0]), jnp.exp(end[1])]
     columns = jnp.concatenate([run, jnp.exp(run), jnp.zeros((112, 256), F32)], 0).T
 
+    px_first(0).wait()
+    sx_first(0).wait()
+    for vy in (1, 3):
+        sx_second(vy).wait()
+        px_second(vy).wait()
+    cbuf[...] = (
+        (sx[0, 384:400] + sx1[0, 384:400]) + (sx2[1, 384:400] + sx2[3, 384:400])
+    ).astype(F32)
+
+    def total_x(c0, n):
+        cols = slice(c0, c0 + n)
+        out = px[0, :, cols].astype(F32) + px1[0, :, cols].astype(F32)
+        for vy in (1, 3):
+            out = out + px2[vy, :, cols].astype(F32)
+        return out.astype(BF).astype(F32)
+
+    def conv(values, taps, bias, cache):
+        n = values.shape[1]
+        tok = lax.broadcasted_iota(jnp.int32, (256, n), 0)
+        out = bias + taps[3:4] * values
+        for lag in range(1, 4):
+            earlier = pltpu.roll(values, lag, 0)
+            for i in range(2):
+                for o in range(lag):
+                    at = o if i == 0 else start + o
+                    earlier = jnp.where(tok == at, cache(i, 3 + o - lag), earlier)
+            out = out + taps[3 - lag : 4 - lag] * earlier
+        return jax.nn.silu(out).astype(BF)
+
+    def cache_b(i, m):
+        e = i * 3 + m
+        return cbuf[12 + e // 2 : 13 + e // 2, e % 2 * 128 : e % 2 * 128 + 128] * live[i]
+
+    bcg[0] = conv(total_x(512, 128), cbw_ref[...], cbb_ref[...], cache_b)
+    shares = []
+    for q in range(1, 4):
+        copy = pltpu.make_async_remote_copy(
+            src_ref=bcg.at[0], dst_ref=bcg.at[q], send_sem=b_send.at[q], recv_sem=b_recv.at[q],
+            device_id={"req": r, "wide": quad_w[q]}, device_id_type=MESH,
+        )
+        copy.start()
+        shares.append(copy)
+
+    for half in range(2):
+        def cache_x(i, m):
+            e = 2 * (i * 3 + m) + half
+            return cbuf[e : e + 1, :] * live[i]
+
+        cols = slice(half * 256, half * 256 + 256)
+        xs = conv(total_x(half * 256, 256), cxw_ref[:, cols], cxb_ref[:, cols], cache_x)
+        xsb[:, cols] = xs
+        xst_ref[cols, :] = xs.astype(F32).T
+
     for copy in shares:
         copy.wait()
 
@@ -482,7 +486,7 @@
     vm = pl.BlockSpec(memory_space=pltpu.VMEM)
     sm = pl.BlockSpec(memory_space=pltpu.SMEM)
     dma = pltpu.SemaphoreType.DMA
-    n_q = 7 + 7 + 6
+    n_q = 3 + 14 + 14 + 2
     return pl.pallas_call(
         project_kernel,
         out_shape=(

time: 113 us -> 111 us (0.982)
  Pallas kernels: 96.3 us -> 95.1 us
    pallas_call x1, Pallas kernels: 96.3 us -> 95.1 us  [project(): pl.pallas_call(project_kernel, out_shape=(jax.ShapeDtypeStruct((256, 512)...]
where the time goes in v4:
time: 111 us
  Pallas kernels  95.1 us (86%)
  local copies, waits for them, and re-layouts  7.88 us (7%)
  waiting for transfers between devices  4.67 us (4%)
  starting transfers between devices  2.75 us (2%)
    pallas_call x1, Pallas kernels, project(): pl.pallas_call(project_kernel, out_shape=(jax.ShapeDtypeStruct((256, 512)...  95.1 us
    unnamed x5, local copies, waits for them, and re-layouts  7.88 us
    ppermute x1, waiting for transfers between devices, on_device(): x_t = lax.ppermute(x_in, ('wide', 'req'), route)  4.67 us
    ppermute x1, starting transfers between devices, on_device(): x_t = lax.ppermute(x_in, ('wide', 'req'), route)  2.75 us
  transfers between devices with their start and end apart: 1, of which 1 were waited for; matrix products, arithmetic and copies ran while one was open for 3% of the time, Pallas kernels for 0%

profile of v4, /device:TPU:101, one launch (start us, length us, event | category | flops | bytes accessed | tf_op | source)
XLA Modules:
  0.0 111.1 jit_solution(550502730694381251)
XLA Ops:
  0.6 2.7 %collective-permute-start = (bf16[256,256]{1,0:T(8,128)(2,1)}, bf16[256,256]{1,0:T(8,128)(2,1)S(1)}, u32[]{:S(2)}, u32[]{:S(2)}) collective-permute-start(bf16[256,256]{1,0:T(8,128)(2,1)} %param.18), channel_id=1, source_target_pairs={{0,0},{8,8},{16,16},{24,24},{32,33},{40,41},{48,49},{56,57},{64,66... | collective-permute-start | bytes 393224 | tf_op jit(solution)/shard_map/ppermute | solution.py:552
  3.4 3.3 %copy.22 = bf16[1024,2,512]{2,0,1:T(8,128)(2,1)} copy(bf16[1024,2,512]{2,1,0:T(2,128)(2,1)} %param.19) | data formatting | bytes 4194304 | tf_op args[1]
  6.6 4.7 %collective-permute-done.x_ref = bf16[256,256]{1,0:T(8,128)(2,1)S(1)} collective-permute-done((bf16[256,256]{1,0:T(8,128)(2,1)}, bf16[256,256]{1,0:T(8,128)(2,1)S(1)}, u32[]{:S(2)}, u32[]{:S(2)}) %collective-permute-start) | collective-permute-done | bytes 131104 | tf_op jit(solution)/shard_map/ppermute | solution.py:552
  11.3 0.0 copy-start
  11.3 0.7 copy-done
  12.0 95.1 %project.1 = (bf16[256,512]{1,0:T(8,128)(2,1)}, f32[2,512,256]{2,1,0:T(8,128)}) custom-call(bf16[256,256]{1,0:T(8,128)(2,1)} %copy-done, bf16[2,1024,512]{2,1,0:T(8,128)(2,1)} %bitcast.11, bf16[1024,128]{1,0:T(8,128)(2,1)} %wbc_ref.1, bf16[8,1024]{1,0:T(8,128)(2,1)} %bitcast.15, s32[16]{0:T(128)} %slot_ref.1, s32[1,2]{1,0:T(1,128)} %start_ref.1, ...), custom_call_target="tpu_custom_call" | custom-call | tf_op jit(solution)/shard_map/project/pallas_call | solution.py:490
  107.1 1.7 %copy.25 = bf16[256,512]{1,0:T(8,128)(2,1)} copy(bf16[256,512]{1,0:T(8,128)(2,1)} %get-tuple-element.8) | data formatting | bytes 524288
  108.8 2.3 %copy.26 = f32[2,8,64,256]{3,2,1,0:T(8,128)} copy(f32[2,8,64,256]{3,2,1,0:T(8,128)} %bitcast.13) | data formatting | bytes 2097152
Async XLA Ops:
  0.6 10.7 %collective-permute-start = (bf16[256,256]{1,0:T(8,128)(2,1)}, bf16[256,256]{1,0:T(8,128)(2,1)S(1)}, u32[]{:S(2)}, u32[]{:S(2)}) collective-permute-start(bf16[256,256]{1,0:T(8,128)(2,1)} %param.18), channel_id=1, source_target_pairs={{0,0},{8,8},{16,16},{24,24},{32,33},{40,41},{48,49},{56,57},{64,66... | collective-permute-start | bytes 393224 | tf_op jit(solution)/shard_map/ppermute | solution.py:552
  11.3 0.7 copy-start
